TPU v7x, 32 devices: a whole 2x2x4 slice. The times are simulated.
32 devices in a mesh: groups: 2 (over y), shard: 16 (over z, x, core).
Axes of the slice: x: 2, y: 2, z: 4, core: 2. Of those that a mesh axis runs over, the one named last changes fastest.
Arguments:
- grad_out: bfloat16 [4, 4096, 2048], P('groups', 'shard'), parts along dimension 0, may hold values from -6 to 6
- saved_input: bfloat16 [4, 4096, 2048], P('groups', 'shard'), parts along dimension 0, may hold values from -6 to 6
- lengths: int32 [4], P('groups'), parts along dimension 0, may hold values from 1024 to 4096, as said below
- kernel: float32 [31, 2048], replicated, may hold values from -1 to 1
- gain: float32 [2048], replicated, may hold values from 0.1 to 1.9
- bias: float32 [2048], replicated, may hold values from -4 to 4
- proj_weight: bfloat16 [2048, 2048], P('shard'), may hold values from -0.125 to 0.125
Outputs:
- input_grad: bfloat16 [4, 4096, 2048], P('groups', 'shard'), parts along dimension 0
- proj_grad: float32 [4096, 2048], P(('groups', 'shard')), parts along dimension 0
- kernel_grad: float32 [62, 2048], P('groups', 'shard'), parts along dimension 0
- norm_grads: float32 [4, 2048], P('groups', 'shard'), parts along dimension 0
There are 2 independent parts, one for each index of `groups`. A program takes and returns all parts, laid end to end along the dimension named above; an argument that names none is the same for every part. Nothing has to cross between parts.
Inputs may be any that keep to these rules, and one draw needn't show every extreme that they name: `lengths`: one utterance of every microbatch is live over all 4096 frames.
All inputs are finite; a program needn't handle non-finite values.
Results may differ from a plain program's by a relative error of at most 0.0051.
Values may be sent and summed in bfloat16 or wider, within the bound.
No kernel may reach another device: no remote copies, remote signals or barrier semaphores. Data moves between devices by JAX's collectives and lax.ppermute only.
A program may use at most 128 MiB of HBM per device.

v0:
```python
import functools

import jax
import jax.numpy as jnp
import numpy as np
from jax import lax
from jax.experimental import pallas as pl
from jax.experimental.pallas import tpu as pltpu
from jax.sharding import PartitionSpec as P


LANES = 128
CORES = 2
VMEM_LIMIT = 56 * 1024 * 1024
POINTS = 256


def cost(micros):
    return pl.CostEstimate(flops=0, transcendentals=0, bytes_accessed=int(micros * 3.6e6))


def extended(block, width):
    count = lax.axis_size("shard")
    forward = [(i, i + 1) for i in range(count - 1)]
    backward = [(target, source) for source, target in forward]
    low = lax.ppermute(block[:, block.shape[1] - width :], "shard", forward)
    high = lax.ppermute(block[:, :width], "shard", backward)
    return jnp.concatenate([low, block, high], axis=1)


def frame_mask(lengths, offset, count):
    position = offset + jnp.arange(count, dtype=jnp.int32)
    return (position[None, :] < lengths[:, None])[:, :, None]


def plain_shards(grad_out, saved_input, lengths, kernel, gain, bias, proj_weight):
    batches, frames, model_width = grad_out.shape
    tap_count = kernel.shape[0]
    half_span = (tap_count - 1) // 2
    offset = lax.axis_index("shard") * frames
    norm_scale = lax.rsqrt(jnp.sum(lengths).astype(jnp.float32))
    own_mask = frame_mask(lengths, offset, frames)
    masked_in = jnp.where(own_mask, saved_input, jnp.zeros_like(saved_input))
    masked_grad = jnp.where(own_mask, grad_out, jnp.zeros_like(grad_out))
    in_ext = extended(masked_in, half_span)
    conv = jnp.zeros(grad_out.shape, jnp.float32)
    for tap in range(tap_count):
        conv = conv + kernel[tap] * in_ext[:, tap : tap + frames].astype(jnp.float32)
    pre_act = gain * conv + bias
    gate_sig = jax.nn.sigmoid(pre_act)
    activated = (pre_act * gate_sig).astype(jnp.bfloat16)
    rows = masked_grad.reshape(batches * frames, model_width)
    weight = lax.all_gather(proj_weight, "shard", axis=0, tiled=True)
    act_grad = lax.dot_general(
        rows, weight, (((1,), (1,)), ((), ())), preferred_element_type=jnp.float32
    ).reshape(batches, frames, model_width)
    pre_grad = act_grad * gate_sig * (1.0 + pre_act * (1.0 - gate_sig))
    conv_grad = (pre_grad * gain).astype(jnp.bfloat16)
    grad_ext = extended(conv_grad, half_span)
    back_sum = jnp.zeros(grad_out.shape, jnp.float32)
    grad_float = conv_grad.astype(jnp.float32)
    tap_rows = []
    for tap in range(tap_count):
        begin = 2 * half_span - tap
        back_sum = back_sum + kernel[tap] * grad_ext[:, begin : begin + frames].astype(jnp.float32)
        tap_rows.append(
            jnp.sum(in_ext[:, tap : tap + frames].astype(jnp.float32) * grad_float, axis=(0, 1))
        )
    input_grad = jnp.where(own_mask, back_sum, 0.0).astype(jnp.bfloat16)
    tap_rows.append(jnp.sum(pre_grad * conv, axis=(0, 1)))
    tap_rows.append(jnp.sum(pre_grad, axis=(0, 1)))
    stats = jnp.stack(tap_rows, 0) * norm_scale
    summed = lax.psum_scatter(stats, "shard", scatter_dimension=1, tiled=True)
    product = lax.dot_general(
        activated.reshape(batches * frames, model_width),
        rows,
        (((0,), (0,)), ((), ())),
        preferred_element_type=jnp.float32,
    )
    proj_grad = lax.psum_scatter(product * norm_scale, "shard", scatter_dimension=0, tiled=True)
    return (input_grad, proj_grad, summed[:tap_count], summed[tap_count:])


class Plan:
    def __init__(self, count, groups, batches, frames, model_width, tap_count):
        self.count = count
        self.chips = count // CORES
        self.rounds = self.chips // 2
        self.batches = batches
        self.frames = frames
        self.chip_frames = CORES * frames
        self.width = model_width
        self.block = model_width // count
        self.taps = tap_count
        self.half = (tap_count - 1) // 2
        self.ghalo = -(-self.half // 16) * 16
        self.xhalo = 2 * self.ghalo
        self.ext = self.chip_frames + 2 * self.ghalo
        self.xext = self.chip_frames + 2 * self.xhalo
        self.tap_rows = -(-tap_count // 16) * 16
        self.stat_rows = self.tap_rows + 8
        self.weight_parts = 2 if groups == 2 else 1
        self.pairs = [(h, 1 - h) for h in range(self.rounds, 0, -1)]
        self.conv_windows = windows(self.ext, self.xhalo - self.ghalo - self.half + tap_count)
        self.back_windows = windows(self.chip_frames, self.ghalo + self.half + 1)

    def window_rows(self, found):
        return found[0] * (found[1] - 1) + POINTS

    def block_slot(self, step, side):
        return 3 + self.batches + 2 * step + side

    def usable(self):
        return (
            self.count % (2 * CORES) == 0
            and self.block == LANES
            and self.block * self.count == self.width
            and self.frames % 128 == 0
            and self.frames >= self.xhalo
            and self.taps % 2 == 1
            and 4 * self.ghalo <= POINTS // 2
            and self.window_rows(self.conv_windows) >= self.xext
            and self.window_rows(self.back_windows) >= self.ext
            and self.window_rows(self.conv_windows)
            >= self.xhalo + self.window_rows(self.back_windows) - self.back_windows[0]
            and self.chips == 8
            and self.batches == 2
        )

    def chip_at(self, position):
        half = self.chips // 2
        return jnp.where(position < half, 2 * position, 2 * (self.chips - 1 - position) + 1)

    def position_of(self, chip):
        return jnp.where(chip % 2 == 0, chip // 2, self.chips - 1 - chip // 2)

    def ring(self):
        half = self.chips // 2
        order = [2 * i for i in range(half)] + [2 * i + 1 for i in reversed(range(half))]
        forward = []
        for core in range(CORES):
            for i in range(self.chips):
                source, target = order[i], order[(i + 1) % self.chips]
                forward.append((CORES * source + core, CORES * target + core))
        return forward, [(t, s) for s, t in forward]

    def edges(self):
        pairs = []
        for chip in range(self.chips - 1):
            last, first = CORES * chip + 1, CORES * (chip + 1)
            pairs += [(last, first), (first, last)]
        return pairs

    def edges_like(self):
        pairs = []
        for chip in range(self.chips - 1):
            pairs.append((CORES * chip + 1, CORES * (chip + 1) + 1))
            pairs.append((CORES * (chip + 1), CORES * chip))
        return pairs

    def partners(self):
        return [(s, s ^ 1) for s in range(self.count)]


def sigmoid(value):
    return 0.5 * jnp.tanh(0.5 * value) + 0.5


def split(value):
    high = value.astype(jnp.bfloat16)
    return high, (value - high.astype(jnp.float32)).astype(jnp.bfloat16)


def split_matrix(matrix):
    high = matrix.astype(jnp.bfloat16)
    return high, (matrix - high.astype(np.float64)).astype(jnp.bfloat16)


def transforms(plan):
    time = np.arange(POINTS)
    theta = np.pi * (2 * np.arange(POINTS // 2) + 1) / POINTS
    angle = theta[:, None] * time[None, :]
    direct = np.concatenate([np.cos(angle), -np.sin(angle)], 0)
    inverse = direct.T * (2.0 / POINTS)

    def spectrum(lags):
        phase = theta[:, None] * lags[None, :]
        matrix = np.concatenate([np.cos(phase), np.sin(phase)], 0)
        return np.pad(matrix, ((0, 0), (0, plan.tap_rows - plan.taps)))

    taps = np.arange(plan.taps)
    back_lags = plan.ghalo + plan.half - taps
    lag_rows = np.pad(inverse[back_lags], ((0, plan.tap_rows - plan.taps), (0, 0)))
    half = lambda m: m.astype(jnp.bfloat16)
    conv_lags = plan.xhalo - plan.ghalo - plan.half + taps
    return (
        half(direct),
        half(inverse),
        np.stack(split_matrix(spectrum(conv_lags))),
        np.stack(split_matrix(spectrum(back_lags))),
        np.stack(split_matrix(lag_rows)),
        half(direct * (time < plan.back_windows[0])),
    )


def taps_spectrum(t_ref, k_ref):
    high, low = split(jnp.concatenate([k_ref[0][...], k_ref[1][...]], axis=1))
    dot = functools.partial(jnp.dot, preferred_element_type=jnp.float32)
    return dot(t_ref[0], high) + dot(t_ref[1], high) + dot(t_ref[0], low)


def to_spectrum(direct_ref, window):
    return jnp.dot(direct_ref[...], window, preferred_element_type=jnp.float32)


def from_spectrum(inverse_ref, rows, parts, slot):
    return jnp.dot(inverse_ref[:rows, :], parts[slot], preferred_element_type=jnp.float32)


def windows(rows_out, reach):
    count = -(-rows_out // ((POINTS - reach) // 16 * 16))
    return -(-rows_out // count // 16) * 16, count


STEP = 16
HALF = POINTS // 2


def spectral_product(spec, taps, parts, slot):
    for row in range(0, HALF, STEP):
        up, down = slice(row, row + STEP), slice(HALF + row, HALF + row + STEP)
        re, im, kr, ks = spec[slot, up, :], spec[slot, down, :], taps[up, :], taps[down, :]
        parts[slot, up, :] = (re * kr - im * ks).astype(jnp.bfloat16)
        parts[slot, down, :] = (re * ks + im * kr).astype(jnp.bfloat16)


def conv_body(plan, info, *refs):
    own_x, other_x, near_x, far_x, k_ref, gain_ref, bias_ref = (
        refs[2 * i : 2 * i + 2] for i in range(7)
    )
    direct, inverse, t_ref, own_g, other_g = refs[14:19]
    conv_ref, x_ref, out_f, out_b, spec, taps, parts, act, acc = refs[19:]
    each, count = plan.conv_windows
    f, xh, gh, cf = plan.frames, plan.xhalo, plan.ghalo, plan.chip_frames
    b = pl.program_id(0)
    core, offset, live = info[0], info[1], info[3 + b]

    @pl.when(b == 0)
    def _():
        taps[...] = taps_spectrum(t_ref, k_ref)

    def put(row, pair):
        for part in range(0, pair[0].shape[1], STEP):
            position = lax.broadcasted_iota(jnp.int32, (STEP, LANES), 0) + (
                offset - xh + row + part
            )
            keep = jnp.where(position < live, 1.0, 0.0).astype(jnp.bfloat16)
            for side in range(2):
                lanes = slice(side * LANES, (side + 1) * LANES)
                x_ref[0, row + part : row + part + STEP, lanes] = (
                    pair[side][0, part : part + STEP, :] * keep
                )

    @pl.when(core == 0)
    def _():
        put(0, near_x)
        put(xh, own_x)
        put(xh + f, other_x)
        put(xh + 2 * f, far_x)

    @pl.when(core != 0)
    def _():
        put(0, far_x)
        put(xh, other_x)
        put(xh + f, own_x)
        put(xh + 2 * f, near_x)

    x_ref[0, plan.xext :, :] = jnp.zeros((x_ref.shape[1] - plan.xext, 2 * LANES), jnp.bfloat16)

    for j in range(count):
        spec[j] = to_spectrum(direct, x_ref[0, j * each : j * each + POINTS, :])
    for j in range(count):
        spectral_product(spec, taps, parts, j)
        rows = min(each, plan.ext - j * each)
        conv_ref[0, j * each : j * each + rows, :] = from_spectrum(inverse, rows, parts, j)

    for i in range(cf // LANES):
        for side in range(2):
            lanes = slice(side * LANES, (side + 1) * LANES)
            begin = gh + i * LANES
            conv = conv_ref[0, begin : begin + LANES, lanes]
            pre = gain_ref[side][...] * conv + bias_ref[side][...]
            position = lax.broadcasted_iota(jnp.int32, (LANES, LANES), 0) + (offset + i * LANES)
            value = jnp.where(position < live, pre * sigmoid(pre), 0.0)
            act[lanes, i * LANES : (i + 1) * LANES] = value.T.astype(jnp.bfloat16)

    own = pl.multiple_of(core * f, f)
    other = pl.multiple_of((1 - core) * f, f)

    def product(columns):
        dot = functools.partial(jnp.dot, preferred_element_type=jnp.float32)
        return dot(act[:, pl.ds(own, f)], own_g[0, :, columns]) + dot(
            act[:, pl.ds(other, f)], other_g[0, :, columns]
        )

    tiles = [slice(c, c + 2 * LANES) for c in range(0, plan.width, 2 * LANES)]

    @pl.when(b == 0)
    def _():
        for columns in tiles:
            acc[:, columns] = product(columns)

    @pl.when(b != 0)
    def _():
        for columns in tiles:
            total = acc[:, columns] + product(columns)
            if plan.batches > 2:
                acc[:, columns] = total
            out_f[:, columns] = total[:LANES].astype(out_f.dtype)
            out_b[:, columns] = total[LANES:].astype(out_b.dtype)


def pair_specs(plan, step, shape, index):
    return [
        pl.BlockSpec(
            shape, lambda b, info, at=plan.block_slot(step, side): index(b, info[at])
        )
        for side in range(2)
    ]


def whole(array):
    return pl.BlockSpec(
        array.shape, lambda *_: (0,) * array.ndim, pipeline_mode=pl.Buffered(1)
    )


def conv_call(plan, step, info, x, xp, xa, xb, g, gp, kernel, gain, bias, consts, kind):
    bt = plan.batches
    flat = lambda b, block: (0, block)
    fixed = lambda b, info: (0, 0)
    direct, inverse, t_conv = consts[:3]
    wide = 2 * LANES
    slots = plan.conv_windows[1]
    specs = functools.partial(pair_specs, plan, step)
    frames, halo = (1, plan.frames, LANES), (1, plan.xhalo, LANES)
    by_batch = lambda b, block: (b, 0, block)
    by_chip = lambda b, block: (b, 0, block // CORES)
    x_rows = plan.window_rows(plan.conv_windows)
    return pl.pallas_call(
        functools.partial(conv_body, plan),
        grid_spec=pltpu.PrefetchScalarGridSpec(
            num_scalar_prefetch=1,
            grid=(bt,),
            in_specs=specs(frames, by_batch)
            + specs(frames, by_batch)
            + specs(halo, by_chip)
            + specs(halo, by_chip)
            + specs((plan.tap_rows, LANES), flat)
            + specs((1, LANES), flat)
            + specs((1, LANES), flat)
            + [whole(direct), whole(inverse), whole(t_conv)]
            + [pl.BlockSpec((1, plan.frames, plan.width), lambda b, info: (b, 0, 0))] * 2,
            out_specs=[
                pl.BlockSpec((1, plan.ext, wide), lambda b, info: (b, 0, 0)),
                pl.BlockSpec((1, x_rows, wide), lambda b, info: (b, 0, 0)),
                pl.BlockSpec((LANES, plan.width), fixed),
                pl.BlockSpec((LANES, plan.width), fixed),
            ],
            scratch_shapes=[
                pltpu.VMEM((slots, POINTS, wide), jnp.float32),
                pltpu.VMEM((POINTS, wide), jnp.float32),
                pltpu.VMEM((slots, POINTS, wide), jnp.bfloat16),
                pltpu.VMEM((wide, plan.chip_frames), jnp.bfloat16),
                pltpu.VMEM((wide, plan.width), jnp.float32),
            ],
        ),
        out_shape=[
            jax.ShapeDtypeStruct((bt, plan.ext, wide), jnp.float32),
            jax.ShapeDtypeStruct((bt, x_rows, wide), jnp.bfloat16),
            jax.ShapeDtypeStruct((LANES, plan.width), kind),
            jax.ShapeDtypeStruct((LANES, plan.width), kind),
        ],
        compiler_params=pltpu.CompilerParams(vmem_limit_bytes=VMEM_LIMIT),
        cost_estimate=cost(6.0),
        name="conv",
    )(info, x, x, xp, xp, xa, xa, xb, xb, kernel, kernel, gain, gain, bias, bias,
      direct, inverse, t_conv, g, gp)


def back_body(plan, steps, sources, info, *refs):
    pairs = len(steps)
    mg_ref = refs[0]
    k_refs, gain_refs, bias_refs = (
        refs[1 + 2 * pairs * i : 1 + 2 * pairs * (i + 1)] for i in range(3)
    )
    refs = refs[1 + 6 * pairs :]
    conv_refs, x_refs, w_refs = refs[:pairs], refs[pairs : 2 * pairs], refs[2 * pairs : -25]
    direct, segment, inverse, t_ref, lag_ref = refs[-25:-20]
    (own_ref, send_ref, stat_ref, weight, conv_buf, x_buf, ag, gs, tail, spec, xspec, taps,
     cross, parts, os, sums, flat, w_sem, c_sem, x_sem) = refs[-20:]
    core, offset, side_y = info[0], info[1], info[2]
    f, xh, gh, cf, ext = plan.frames, plan.xhalo, plan.ghalo, plan.chip_frames, plan.ext
    each, count = plan.back_windows
    turn, b = pl.program_id(0), pl.program_id(1)
    live = info[3 + b]

    def weight_copies(pair):
        made = []
        for n, (array, part, target, begin, rows) in enumerate(sources[pair]):
            first, into = begin, target * LANES
            if part is not None:
                into = pl.multiple_of(target * LANES + (side_y + part) % 2 * rows, rows)
            made.append(
                pltpu.make_async_copy(
                    w_refs[array].at[pl.ds(first, rows), :],
                    weight.at[pair, pl.ds(into, rows), :],
                    w_sem.at[pair, n],
                )
            )
        return made

    def conv_copies(pair):
        return [
            pltpu.make_async_copy(conv_refs[pair].at[i], conv_buf.at[pair, i], c_sem.at[pair, i])
            for i in range(plan.batches)
        ] + [
            pltpu.make_async_copy(x_refs[pair].at[i], x_buf.at[pair, i], x_sem.at[pair, i])
            for i in range(plan.batches)
        ]

    @pl.when((turn == 0) & (b == 0))
    def _():
        for pair in range(pairs):
            for copy in weight_copies(pair) + conv_copies(pair):
                copy.start()
        gs[ext:, :] = jnp.zeros((gs.shape[0] - ext, 2 * LANES), jnp.bfloat16)
        tail[...] = jnp.zeros_like(tail)

    for pair in range(pairs):

        @pl.when((turn == pair) & (b == 0))
        def _():
            taps[...] = taps_spectrum(t_ref, k_refs[2 * pair : 2 * pair + 2])
            for row, pick in ((0, gain_refs), (8, bias_refs)):
                for side in range(2):
                    lanes = slice(side * LANES, (side + 1) * LANES)
                    flat[row : row + 8, lanes] = jnp.broadcast_to(
                        pick[2 * pair + side][...], (8, LANES)
                    )
            cross[...] = jnp.zeros_like(cross)
            sums[...] = jnp.zeros_like(sums)
            for copy in weight_copies(pair) + conv_copies(pair):
                copy.wait()

    last_rows = cf - (count - 1) * each
    for j in range(count):
        begin = xh + j * each
        if j < count - 1:
            window = x_buf[turn, b, begin : begin + POINTS, :]
        else:
            tail[:last_rows, :] = x_buf[turn, b, begin : begin + last_rows, :]
            window = tail[...]
        xspec[j] = to_spectrum(segment, window)

    ag[...] = lax.dot_general(
        mg_ref[0], weight[turn], (((1,), (1,)), ((), ())), preferred_element_type=jnp.float32
    )
    gain, bias = flat[:1, :], flat[8:9, :]

    gain_sum = jnp.zeros((8, 2 * LANES), jnp.float32)
    bias_sum = jnp.zeros((8, 2 * LANES), jnp.float32)
    for row in range(0, ext, STEP):
        conv = conv_buf[turn, b, row : row + STEP, :]
        pre = gain * conv + bias
        sig = sigmoid(pre)
        value = ag[row : row + STEP, :] * sig * (1.0 + pre * (1.0 - sig))
        gs[row : row + STEP, :] = (value * gain).astype(jnp.bfloat16)
        if gh <= row < gh + cf:
            fold = lambda v: jnp.sum(v.reshape(STEP // 8, 8, 2 * LANES), axis=0)
            gain_sum = gain_sum + fold(value * conv)
            bias_sum = bias_sum + fold(value)
    sums[0] += gain_sum
    sums[1] += bias_sum

    for j in range(count):
        spec[j] = to_spectrum(direct, gs[j * each : j * each + POINTS, :])
    for j in range(count):
        spectral_product(spec, taps, parts, j)
        rows = min(each, cf - j * each)
        value = from_spectrum(inverse, rows, parts, j)
        position = offset + j * each + lax.broadcasted_iota(jnp.int32, value.shape, 0)
        os[j * each : j * each + rows, :] = jnp.where(position < live, value, 0.0).astype(
            jnp.bfloat16
        )
    for row in range(0, HALF, STEP):
        up, down = slice(row, row + STEP), slice(HALF + row, HALF + row + STEP)
        total_r, total_i = cross[up, :], cross[down, :]
        for j in range(count):
            re, im, xr, xi = spec[j, up, :], spec[j, down, :], xspec[j, up, :], xspec[j, down, :]
            total_r = total_r + re * xr + im * xi
            total_i = total_i + im * xr - re * xi
        cross[up, :] = total_r
        cross[down, :] = total_i

    @pl.when(core == 0)
    def _():
        own_ref[0, 0] = os[:f]
        send_ref[0, 0] = os[f:]

    @pl.when(core != 0)
    def _():
        own_ref[0, 0] = os[f:]
        send_ref[0, 0] = os[:f]

    @pl.when(b == plan.batches - 1)
    def _():
        high, low = split(cross[...])
        dot = functools.partial(jnp.dot, preferred_element_type=jnp.float32)
        stat_ref[0, : plan.tap_rows] = (
            dot(lag_ref[0], high) + dot(lag_ref[1], high) + dot(lag_ref[0], low)
        )
        total = [jnp.sum(sums[i], axis=0, keepdims=True) for i in range(2)]
        pad = jnp.zeros((plan.stat_rows - plan.tap_rows - 2, 2 * LANES), jnp.float32)
        stat_ref[0, plan.tap_rows :] = jnp.concatenate(total + [pad], axis=0)


def back_call(plan, steps, info, mg, sources, arrays, convs, xs, kernel, gain, bias, consts):
    bt, pairs = plan.batches, len(steps)
    direct, inverse, _, t_back, lags, segment = consts
    wide = 2 * LANES
    slots = plan.back_windows[1]
    any_space = pl.BlockSpec(memory_space=pl.ANY)

    def by_block(shape):
        return [
            pl.BlockSpec(
                shape, lambda p, b, info, at=plan.block_slot(step, side): (0, info[at]),
                pipeline_mode=pl.Buffered(1),
            )
            for step in steps for side in range(2)
        ]

    each = lambda *tail: pl.BlockSpec((1, 1) + tail, lambda p, b, info: (p, b, 0, 0))
    most = max(len(source) for source in sources)
    return pl.pallas_call(
        functools.partial(back_body, plan, steps, sources),
        grid_spec=pltpu.PrefetchScalarGridSpec(
            num_scalar_prefetch=1,
            grid=(pairs, bt),
            in_specs=[
                pl.BlockSpec((1, plan.ext, plan.width), lambda p, b, info: (b, 0, 0)),
            ]
            + by_block((plan.tap_rows, LANES))
            + by_block((1, LANES))
            + by_block((1, LANES))
            + [any_space] * (2 * pairs + len(arrays))
            + [whole(c) for c in (direct, segment, inverse, t_back, lags)],
            out_specs=[
                each(plan.frames, wide),
                each(plan.frames, wide),
                pl.BlockSpec((1, plan.stat_rows, wide), lambda p, b, info: (p, 0, 0)),
            ],
            scratch_shapes=[
                pltpu.VMEM((pairs, wide, plan.width), jnp.bfloat16),
                pltpu.VMEM((pairs, bt, plan.ext, wide), jnp.float32),
                pltpu.VMEM((pairs, bt, xs[0].shape[1], wide), jnp.bfloat16),
                pltpu.VMEM((plan.ext, wide), jnp.float32),
                pltpu.VMEM((plan.window_rows(plan.back_windows), wide), jnp.bfloat16),
                pltpu.VMEM((POINTS, wide), jnp.bfloat16),
                pltpu.VMEM((slots, POINTS, wide), jnp.float32),
                pltpu.VMEM((slots, POINTS, wide), jnp.float32),
                pltpu.VMEM((POINTS, wide), jnp.float32),
                pltpu.VMEM((POINTS, wide), jnp.float32),
                pltpu.VMEM((slots, POINTS, wide), jnp.bfloat16),
                pltpu.VMEM((plan.chip_frames, wide), jnp.bfloat16),
                pltpu.VMEM((2, 8, wide), jnp.float32),
                pltpu.VMEM((16, wide), jnp.float32),
                pltpu.SemaphoreType.DMA((pairs, most)),
                pltpu.SemaphoreType.DMA((pairs, bt)),
                pltpu.SemaphoreType.DMA((pairs, bt)),
            ],
        ),
        out_shape=[
            jax.ShapeDtypeStruct((pairs, bt, plan.frames, wide), jnp.bfloat16),
            jax.ShapeDtypeStruct((pairs, bt, plan.frames, wide), jnp.bfloat16),
            jax.ShapeDtypeStruct((pairs, plan.stat_rows, wide), jnp.float32),
        ],
        compiler_params=pltpu.CompilerParams(vmem_limit_bytes=VMEM_LIMIT),
        cost_estimate=cost(6.0 * pairs),
        name="back",
    )(info, mg, *[kernel] * 2 * pairs, *[gain] * 2 * pairs, *[bias] * 2 * pairs,
      *convs, *xs, *arrays, direct, segment, inverse, t_back, lags)


def place_body(plan, calls, info, *refs):
    out_ref = refs[-1]
    for i, ref in enumerate(refs[:-1]):
        for turn, step in enumerate(calls[i // 2]):
            for side in range(2):
                block = info[plan.block_slot(step, side)]
                if i % 2:
                    block = block + 1 - 2 * info[0]
                column = pl.multiple_of(block * LANES, LANES)
                lanes = slice(side * LANES, (side + 1) * LANES)
                out_ref[:, :, pl.ds(column, LANES)] = ref[turn, :, :, lanes]


def place_call(plan, calls, info, arrays):
    shape = (plan.batches, plan.frames, plan.width)
    return pl.pallas_call(
        functools.partial(place_body, plan, calls),
        grid_spec=pltpu.PrefetchScalarGridSpec(
            num_scalar_prefetch=1,
            grid=(1,),
            in_specs=[whole(array) for array in arrays],
            out_specs=pl.BlockSpec(shape, lambda g, info: (0, 0, 0)),
        ),
        out_shape=jax.ShapeDtypeStruct(shape, jnp.bfloat16),
        compiler_params=pltpu.CompilerParams(vmem_limit_bytes=VMEM_LIMIT),
        cost_estimate=cost(3.0),
        name="place",
    )(info, *arrays)


def deal_body(plan, calls, info, *refs):
    out_ref = refs[-1]
    for steps, ref in zip(calls, refs[:-1]):
        for turn, step in enumerate(steps):
            for side in range(2):
                chip = info[plan.block_slot(step, side)] // CORES
                out_ref[chip] = ref[turn, :, side * LANES : (side + 1) * LANES]


def deal_call(plan, calls, info, arrays):
    shape = (plan.chips, plan.stat_rows, LANES)
    return pl.pallas_call(
        functools.partial(deal_body, plan, calls),
        grid_spec=pltpu.PrefetchScalarGridSpec(
            num_scalar_prefetch=1,
            grid=(1,),
            in_specs=[whole(array) for array in arrays],
            out_specs=pl.BlockSpec(shape, lambda g, info: (0, 0, 0)),
        ),
        out_shape=jax.ShapeDtypeStruct(shape, jnp.float32),
        cost_estimate=cost(1.0),
        name="deal",
    )(info, *arrays)


def edge_body(plan, x_first, x_last, g_first, g_last, near_ref, far_ref, g_ref):
    core = lax.axis_index("shard") % CORES

    def take(owner, x_ref, grad_ref):
        for i in range(plan.chips):
            for out, parity in ((near_ref, 1 - owner), (far_ref, owner)):
                column = (CORES * i + parity) * LANES
                out[:, :, i * LANES : (i + 1) * LANES] = x_ref[:, :, column : column + LANES]
        g_ref[...] = grad_ref[...]

    pl.when(core == 0)(lambda: take(0, x_first, g_first))
    pl.when(core != 0)(lambda: take(1, x_last, g_last))


def edge_call(plan, x, g):
    def spec(rows, first):
        shape = (plan.batches, rows, plan.width)
        block = 0 if first else plan.frames // rows - 1
        return pl.BlockSpec(shape, lambda i: (0, block, 0))

    xh, gh = plan.xhalo, plan.ghalo
    half = (plan.batches, xh, plan.width // CORES)
    shapes = [half, half, (plan.batches, gh, plan.width)]
    return pl.pallas_call(
        functools.partial(edge_body, plan),
        grid=(1,),
        in_specs=[spec(xh, True), spec(xh, False), spec(gh, True), spec(gh, False)],
        out_specs=[pl.BlockSpec(shape, lambda i: (0, 0, 0)) for shape in shapes],
        out_shape=[jax.ShapeDtypeStruct(shape, jnp.bfloat16) for shape in shapes],
        cost_estimate=cost(1.0),
        name="edge",
    )(x, x, g, g)


def assemble_body(plan, halo, info, own_ref, other_ref, near_ref, far_ref, out_ref):
    core, offset, live = info[0], info[1], info[3 + pl.program_id(0)]
    f = plan.frames

    def put(row, ref):
        for part in range(0, ref.shape[1], STEP):
            position = lax.broadcasted_iota(jnp.int32, (STEP, LANES), 0) + (
                offset - halo + row + part
            )
            keep = jnp.where(position < live, 1.0, 0.0).astype(jnp.bfloat16)
            for i in range(plan.count):
                lanes = slice(i * LANES, (i + 1) * LANES)
                out_ref[0, row + part : row + part + STEP, lanes] = (
                    ref[0, part : part + STEP, lanes] * keep
                )

    @pl.when(core == 0)
    def _():
        put(0, near_ref)
        put(halo, own_ref)
        put(halo + f, other_ref)
        put(halo + 2 * f, far_ref)

    @pl.when(core != 0)
    def _():
        put(0, far_ref)
        put(halo, other_ref)
        put(halo + f, own_ref)
        put(halo + 2 * f, near_ref)


def assemble_call(plan, info, own, other, near, far):
    halo = near.shape[1]
    spec = lambda n: pl.BlockSpec((1, n, plan.width), lambda b, info: (b, 0, 0))
    return pl.pallas_call(
        functools.partial(assemble_body, plan, halo),
        grid_spec=pltpu.PrefetchScalarGridSpec(
            num_scalar_prefetch=1,
            grid=(plan.batches,),
            in_specs=[spec(plan.frames), spec(plan.frames), spec(halo), spec(halo)],
            out_specs=spec(plan.ext),
        ),
        out_shape=jax.ShapeDtypeStruct((plan.batches, plan.ext, plan.width), jnp.bfloat16),
        compiler_params=pltpu.CompilerParams(vmem_limit_bytes=VMEM_LIMIT),
        cost_estimate=cost(5.0),
        name="assemble",
    )(info, own, other, near, far)


def after(value, *others):
    return lax.optimization_barrier((value, *others))[0]


def ring_shards(plan, grad_out, saved_input, lengths, kernel, gain, bias, proj_weight):
    index = lax.axis_index("shard")
    group = lax.axis_index("groups")
    core, chip = index % CORES, index // CORES
    place = plan.position_of(chip)
    forward, backward = plan.ring()
    offset = chip * plan.chip_frames
    scale = lax.rsqrt(jnp.sum(lengths).astype(jnp.float32))
    pairs = plan.pairs
    far = jnp.asarray([d for pair in pairs for d in pair], jnp.int32)
    owned = CORES * plan.chip_at((place + far + plan.chips) % plan.chips) + core
    info = jnp.concatenate([jnp.stack([core, offset, group]), lengths, owned]).astype(jnp.int32)
    gain2, bias2 = gain.reshape(1, -1), bias.reshape(1, -1)
    taps = jnp.pad(kernel, ((0, plan.tap_rows - plan.taps), (0, 0)))
    consts = [jnp.asarray(c) for c in transforms(plan)]

    x_near, x_far, g_edge = edge_call(plan, saved_input, grad_out)
    xa = lax.ppermute(x_near, "shard", plan.edges())
    xb = lax.ppermute(x_far, "shard", plan.edges_like())
    xp = lax.ppermute(saved_input, "shard", plan.partners())
    mgp = lax.ppermute(grad_out, "shard", plan.partners())

    halved = plan.weight_parts == 2
    piece = LANES // 2
    around = {}
    going = [after(proj_weight, xa, xb)] * 2

    def weight_round(step):
        going[0] = lax.ppermute(going[0], "shard", forward)
        around[-step] = going[0]
        if step < plan.rounds:
            going[1] = lax.ppermute(going[1], "shard", backward)
            around[step] = going[1]
        else:
            around[step] = around.pop(-step)

    convs, xs, products = [], [], []

    def conv_step(step, order):
        conv, x, *product = conv_call(
            plan, step, order, saved_input, xp, xa, xb, grad_out,
            mgp, taps, gain2, bias2, consts, jnp.bfloat16 if step == 0 else jnp.float32,
        )
        convs.append(conv)
        xs.append(x)
        products.append(product)

    def sum_round(step, send, *behind):
        received = (
            lax.ppermute(send[0], "shard", forward), lax.ppermute(send[1], "shard", backward)
        )
        kinds = (jnp.bfloat16, jnp.bfloat16 if step < plan.rounds - 1 else jnp.float32)
        own = lax.optimization_barrier((*products[step], *received, *behind))[:2]
        return [
            (product + value.astype(jnp.float32)).astype(kind)
            for product, value, kind in zip(own, received, kinds)
        ]

    weight_round(1)
    conv_step(0, info)
    g_edge = after(g_edge, products[0][0])
    ga = lax.ppermute(g_edge, "shard", plan.edges())
    gb = lax.ppermute(g_edge, "shard", plan.edges_like())
    conv_step(1, after(info, products[0][0]))
    going = list(lax.optimization_barrier((*going, products[1][0]))[:2])
    if halved:
        going = [lax.dynamic_slice_in_dim(w, group * piece, piece, 0) for w in going]
    weight_round(2)
    mg = assemble_call(plan, after(info, products[1][0]), grad_out, mgp, ga, gb)
    send = sum_round(1, products[0], mg)
    going = list(lax.optimization_barrier((*going, mg))[:2])
    weight_round(3)
    conv_step(2, after(info, products[1][0], *send, mg))
    going = list(lax.optimization_barrier((*going, products[2][0]))[:2])
    weight_round(4)
    conv_step(3, after(info, products[2][0]))
    send = sum_round(2, send, products[3][0])

    arrays = [proj_weight]
    source = {0: [(0, None, 0, LANES)]}

    def keep(array):
        arrays.append(array)
        return len(arrays) - 1

    swap = [
        (g * plan.count + s, (1 - g) * plan.count + s) for g in range(2) for s in range(plan.count)
    ]
    for n, distances in enumerate([[1, -1], [2, -2], [3, -3, 4]]):
        if n == 0 or not halved:
            for d in distances:
                source[d] = [(keep(around[d]), None, 0, LANES)]
            continue
        swapped = keep(
            lax.ppermute(
                jnp.concatenate([around[d] for d in distances], 0),
                ("groups", "shard"), swap,
            )
        )
        for i, d in enumerate(distances):
            source[d] = [(keep(around[d]), 0, 0, piece), (swapped, 1, i * piece, piece)]

    calls = [(3, 2), (1, 0)]
    pieces, stats = [], []
    for steps in calls:
        if steps == calls[-1]:
            send = sum_round(3, send, pieces[0])
        order = after(info, products[-1][0], *send)
        used = sorted({a[0] for step in steps for d in pairs[step] for a in source[d]})
        sources = [
            [
                (used.index(array), part, block, begin, rows)
                for block, d in enumerate(pairs[step])
                for array, part, begin, rows in source[d]
            ]
            for step in steps
        ]
        own, given, stat = back_call(
            plan, steps, order, mg, sources, [arrays[i] for i in used],
            [convs[step] for step in steps], [xs[step] for step in steps],
            taps, gain2, bias2, consts,
        )
        stats.append(stat)
        pieces += [own, lax.ppermute(given, "shard", plan.partners())]
    recv_f = after(lax.ppermute(send[0], "shard", forward), stats[-1])
    proj_grad = (send[1] + recv_f.astype(jnp.float32)) * scale
    full = place_call(plan, calls, info, pieces)

    dealt = deal_call(plan, calls, info, stats)
    groups = [[CORES * p + c for p in range(plan.chips)] for c in range(CORES)]
    summed = jnp.sum(
        lax.all_to_all(dealt, "shard", 0, 0, axis_index_groups=groups), axis=0
    ) * scale
    return (
        full, proj_grad, summed[: plan.taps], summed[plan.tap_rows : plan.tap_rows + 2]
    )


def shards(count, group_count, grad_out, saved_input, lengths, kernel, gain, bias, proj_weight):
    batches, frames, model_width = grad_out.shape
    plan = Plan(count, group_count, batches, frames, model_width, kernel.shape[0])
    args = (grad_out, saved_input, lengths, kernel, gain, bias, proj_weight)
    return ring_shards(plan, *args) if plan.usable() else plain_shards(*args)


def solution(mesh):
    placed = (
        P("groups", "shard", None),
        P("groups", "shard", None),
        P("groups"),
        P(),
        P(),
        P(),
        P("shard", None),
    )

    def body(*args):
        return shards(mesh.shape["shard"], mesh.shape["groups"], *args)

    return jax.shard_map(
        body,
        mesh=mesh,
        in_specs=placed,
        out_specs=(
            P("groups", "shard", None),
            P(("groups", "shard"), None),
            P("groups", "shard"),
            P("groups", "shard"),
        ),
        check_vma=False,
    )
```

profile of v0, /device:TPU:0, one launch (start us, length us, event | category | flops | bytes accessed | tf_op | source)
XLA Modules:
  0.0 166.6 jit_solution(17428215020161289063)
XLA Ops:
  1.3 1.9 %edge.1 = (bf16[2,32,1024]{2,1,0:T(8,128)(2,1)}, bf16[2,32,1024]{2,1,0:T(8,128)(2,1)}, bf16[2,16,2048]{2,1,0:T(8,128)(2,1)}) custom-call(bf16[2,256,2048]{2,1,0:T(8,128)(2,1)} %refs_1_.7, bf16[2,256,2048]{2,1,0:T(8,128)(2,1)} %refs_1_.7, bf16[2,256,2048]{2,1,0:T(8,128)(2,1)} %refs_17_.8, bf16[2,256,2048]{2,1,0:T(8,128)(2,1)} %refs_17_.8), custom_call_target="tpu_custom_call" | custom-call | bytes 3600000 | tf_op jit(solution)/shard_map/edge/pallas_call | solution.py:674
  5.2 7.9 %collective-permute-done.2.refs_6_.refs_7_ = bf16[2,32,1024]{2,1,0:T(8,128)(2,1)S(1)} collective-permute-done((bf16[2,32,1024]{2,1,0:T(8,128)(2,1)}, bf16[2,32,1024]{2,1,0:T(8,128)(2,1)S(1)}, u32[]{:S(2)}, u32[]{:S(2)}) %collective-permute-start.2) | collective-permute-done | bytes 131104 | tf_op jit(solution)/shard_map/ppermute | solution.py:756
  13.1 3.0 %collective-permute-start.10 = (bf16[128,2048]{1,0:T(8,128)(2,1)}, bf16[128,2048]{1,0:T(8,128)(2,1)S(1)}, u32[]{:S(2)}, u32[]{:S(2)}) collective-permute-start(bf16[128,2048]{1,0:T(8,128)(2,1)} %refs_17_.9), channel_id=1, source_target_pairs={{4,0},{8,4},{12,8},{14,12},{10,14},{6,10},{2,6},{0,2},{5,1},{9,5},... | collective-permute-start | bytes 1572872 | tf_op jit(solution)/shard_map/ppermute | solution.py:769
  17.6 1.7 %pad.4.refs_8_.refs_9_.refs_1_.refs_2_.refs_3_.refs_4_ = f32[32,2048]{1,0:T(8,128)} pad(f32[31,2048]{1,0:T(8,128)} %param.17, f32[]{:T(128)} %constant.88.clone.1), padding=0_1x0_0 | pad | bytes 516100 | tf_op jit(solution)/shard_map/jit(_pad)/pad | solution.py:751
  21.3 7.2 %conv.4 = (f32[2,544,256]{2,1,0:T(8,128)}, bf16[2,640,256]{2,1,0:T(8,128)(2,1)}, bf16[128,2048]{1,0:T(8,128)(2,1)}, bf16[128,2048]{1,0:T(8,128)(2,1)}) custom-call(s32[13]{0:T(128)} %concatenate.9.info, bf16[2,256,2048]{2,1,0:T(8,128)(2,1)} %refs_1_.7, bf16[2,256,2048]{2,1,0:T(8,128)(2,1)} %refs_1_.7, bf16[2,256,2048]{2,1,0:T(8,128)(2,1)} %copy-done, ...), custom_call_target="tpu_custom_call" | custom-call | bytes 21600000 | tf_op jit(solution)/shard_map/conv/pallas_call | solution.py:350
  28.5 2.1 %collective-permute-start.4 = (bf16[128,2048]{1,0:T(8,128)(2,1)}, bf16[128,2048]{1,0:T(8,128)(2,1)S(1)}, u32[]{:S(2)}, u32[]{:S(2)}) collective-permute-start(bf16[128,2048]{1,0:T(8,128)(2,1)} %get-tuple-element.51), channel_id=1, source_target_pairs={{0,4},{4,8},{8,12},{12,14},{14,10},{10,6},{6,2},{2,0},{1,5},{5,9},... | collective-permute-start | bytes 1572872 | tf_op jit(solution)/shard_map/ppermute | solution.py:787
  30.6 7.7 %conv.5 = (f32[2,544,256]{2,1,0:T(8,128)}, bf16[2,640,256]{2,1,0:T(8,128)(2,1)}, f32[128,2048]{1,0:T(8,128)}, f32[128,2048]{1,0:T(8,128)}) custom-call(s32[13]{0:T(128)} %concatenate.9.info, bf16[2,256,2048]{2,1,0:T(8,128)(2,1)} %refs_1_.7, bf16[2,256,2048]{2,1,0:T(8,128)(2,1)} %refs_1_.7, bf16[2,256,2048]{2,1,0:T(8,128)(2,1)} %copy-done, ...), custom_call_target="tpu_custom_call" | custom-call | bytes 21600000 | tf_op jit(solution)/shard_map/conv/pallas_call | solution.py:350
  40.4 3.9 %collective-permute-start.13 = (bf16[64,2048]{1,0:T(8,128)(2,1)S(1)}, bf16[64,2048]{1,0:T(8,128)(2,1)S(1)}, u32[]{:S(2)}, u32[]{:S(2)}) collective-permute-start(bf16[64,2048]{1,0:T(8,128)(2,1)S(1)} %constant_dynamic-slice_fusion), channel_id=1, source_target_pairs={{0,4},{4,8},{8,12},{12,14},{14,10},{10,6},{6,2},{2,0},{1,5},{5,9},... | collective-permute-start | bytes 786440 | tf_op jit(solution)/shard_map/ppermute | solution.py:766
  46.5 4.7 %assemble.1.refs_0_ = bf16[2,544,2048]{2,1,0:T(8,128)(2,1)} custom-call(s32[13]{0:T(128)} %concatenate.9.info, bf16[2,256,2048]{2,1,0:T(8,128)(2,1)} %refs_17_.8, bf16[2,256,2048]{2,1,0:T(8,128)(2,1)} %collective-permute-done.3.refs_18_.other_ref, bf16[2,16,2048]{2,1,0:T(8,128)(2,1)} %copy-done.20, bf16[2,16,2048]{2,1,0:T(8,128)(2,1)} %copy-done.21), custom_call_target="tpu_custom_call" | custom-call | bytes 18000000 | tf_op jit(solution)/shard_map/assemble/pallas_call | solution.py:719
  51.3 4.7 %collective-permute-start.8 = (bf16[128,2048]{1,0:T(8,128)(2,1)S(1)}, bf16[128,2048]{1,0:T(8,128)(2,1)S(1)}, u32[]{:S(2)}, u32[]{:S(2)}) collective-permute-start(bf16[128,2048]{1,0:T(8,128)(2,1)S(1)} %add_convert_fusion.4), channel_id=1, source_target_pairs={{0,4},{4,8},{8,12},{12,14},{14,10},{10,6},{6,2},{2,0},{1,5},{5,9},... | collective-permute-start | bytes 1572872 | tf_op jit(solution)/shard_map/ppermute | solution.py:787
  57.1 17.1 %collective-permute-done.12.refs_21_ = bf16[64,2048]{1,0:T(8,128)(2,1)S(1)} collective-permute-done((bf16[64,2048]{1,0:T(8,128)(2,1)S(1)}, bf16[64,2048]{1,0:T(8,128)(2,1)S(1)}, u32[]{:S(2)}, u32[]{:S(2)}) %collective-permute-start.12) | collective-permute-done | bytes 262176 | tf_op jit(solution)/shard_map/ppermute | solution.py:769
  74.3 1.6 collective-permute-start.14
  75.9 1.6 collective-permute-start.19
  78.0 7.6 %conv.6 = (f32[2,544,256]{2,1,0:T(8,128)}, bf16[2,640,256]{2,1,0:T(8,128)(2,1)}, f32[128,2048]{1,0:T(8,128)}, f32[128,2048]{1,0:T(8,128)}) custom-call(s32[13]{0:T(128)} %concatenate.9.info, bf16[2,256,2048]{2,1,0:T(8,128)(2,1)} %refs_1_.7, bf16[2,256,2048]{2,1,0:T(8,128)(2,1)} %refs_1_.7, bf16[2,256,2048]{2,1,0:T(8,128)(2,1)} %copy-done, ...), custom_call_target="tpu_custom_call" | custom-call | bytes 21600000 | tf_op jit(solution)/shard_map/conv/pallas_call | solution.py:350
  85.7 7.8 %conv.7 = (f32[2,544,256]{2,1,0:T(8,128)}, bf16[2,640,256]{2,1,0:T(8,128)(2,1)}, f32[128,2048]{1,0:T(8,128)}, f32[128,2048]{1,0:T(8,128)}) custom-call(s32[13]{0:T(128)} %concatenate.9.info, bf16[2,256,2048]{2,1,0:T(8,128)(2,1)} %refs_1_.7, bf16[2,256,2048]{2,1,0:T(8,128)(2,1)} %refs_1_.7, bf16[2,256,2048]{2,1,0:T(8,128)(2,1)} %copy-done, ...), custom_call_target="tpu_custom_call" | custom-call | bytes 21600000 | tf_op jit(solution)/shard_map/conv/pallas_call | solution.py:350
  95.2 1.6 collective-permute-start.17
  97.4 14.9 %collective-permute-done.20.refs_22_ = bf16[64,2048]{1,0:T(8,128)(2,1)S(1)} collective-permute-done((bf16[64,2048]{1,0:T(8,128)(2,1)S(1)}, bf16[64,2048]{1,0:T(8,128)(2,1)S(1)}, u32[]{:S(2)}, u32[]{:S(2)}) %collective-permute-start.20) | collective-permute-done | bytes 262176 | tf_op jit(solution)/shard_map/ppermute | solution.py:766
  113.8 12.9 %back.2 = (bf16[2,2,256,256]{3,2,1,0:T(8,128)(2,1)}, bf16[2,2,256,256]{3,2,1,0:T(8,128)(2,1)}, f32[2,40,256]{2,1,0:T(8,128)}) custom-call(s32[13]{0:T(128)} %concatenate.9.info, bf16[2,544,2048]{2,1,0:T(8,128)(2,1)} %assemble.1.refs_0_, f32[32,2048]{1,0:T(8,128)} %pad.4.refs_8_.refs_9_.refs_1_.refs_2_.refs_3_.refs_4_, ...), custom_call_target="tpu_custom_call" | custom-call | bytes 43200000 | tf_op jit(solution)/shard_map/back/pallas_call | solution.py:546
  128.1 2.2 %collective-permute-done.21.refs_19_ = bf16[192,2048]{1,0:T(8,128)(2,1)S(1)} collective-permute-done((bf16[192,2048]{1,0:T(8,128)(2,1)S(1)}, bf16[192,2048]{1,0:T(8,128)(2,1)S(1)}, u32[]{:S(2)}, u32[]{:S(2)}) %collective-permute-start.21) | collective-permute-done | bytes 786464 | tf_op jit(solution)/shard_map/ppermute | solution.py:832
  131.2 12.9 %back.3 = (bf16[2,2,256,256]{3,2,1,0:T(8,128)(2,1)}, bf16[2,2,256,256]{3,2,1,0:T(8,128)(2,1)}, f32[2,40,256]{2,1,0:T(8,128)}) custom-call(s32[13]{0:T(128)} %concatenate.9.info, bf16[2,544,2048]{2,1,0:T(8,128)(2,1)} %assemble.1.refs_0_, f32[32,2048]{1,0:T(8,128)} %pad.4.refs_8_.refs_9_.refs_1_.refs_2_.refs_3_.refs_4_, ...), custom_call_target="tpu_custom_call" | custom-call | bytes 43200000 | tf_op jit(solution)/shard_map/back/pallas_call | solution.py:546
  144.0 2.3 %deal.1 = f32[8,40,128]{2,1,0:T(8,128)} custom-call(s32[13]{0:T(128)} %concatenate.9.info, f32[2,40,256]{2,1,0:T(8,128)} %get-tuple-element.93.refs_0_, f32[2,40,256]{2,1,0:T(8,128)} %get-tuple-element.91.refs_1_), custom_call_target="tpu_custom_call" | custom-call | bytes 3600000 | tf_op jit(solution)/shard_map/deal/pallas_call | solution.py:637
  146.3 5.3 %all-to-all-start = ((f32[8,40,128]{2,1,0:T(8,128)}), f32[8,40,128]{2,1,0:T(8,128)S(1)}, u32[]{:S(2)}, u32[]{:S(2)}) async-start(f32[8,40,128]{2,1,0:T(8,128)} %deal.1), calls=%async_computation | async-start | bytes 327680 | tf_op jit(solution)/shard_map/all_to_all | solution.py:869
  153.5 5.7 %all-to-all-done = f32[8,40,128]{2,1,0:T(8,128)S(1)} async-done(((f32[8,40,128]{2,1,0:T(8,128)}), f32[8,40,128]{2,1,0:T(8,128)S(1)}, u32[]{:S(2)}, u32[]{:S(2)}) %all-to-all-start) | async-done | bytes 163872 | tf_op jit(solution)/shard_map/all_to_all | solution.py:869
  162.4 4.1 %place.1 = bf16[2,256,2048]{2,1,0:T(8,128)(2,1)} custom-call(s32[13]{0:T(128)} %concatenate.9.info, bf16[2,2,256,256]{3,2,1,0:T(8,128)(2,1)} %get-tuple-element.76.refs_0_, bf16[2,2,256,256]{3,2,1,0:T(8,128)(2,1)} %copy-done.18, bf16[2,2,256,256]{3,2,1,0:T(8,128)(2,1)} %get-tuple-element.89.refs_2_, bf16[2,2,256,256]{3,2,1,0:T(8,128)(2,1)} %copy-done.19), custom_call_target="tpu_custom_call" | custom-call | bytes 10800000 | tf_op jit(solution)/shard_map/place/pallas_call | solution.py:611
  (105 shorter events, 22.4 us)
Async XLA Ops:
  0.7 19.3 %collective-permute-start = (bf16[2,256,2048]{2,1,0:T(8,128)(2,1)}, bf16[2,256,2048]{2,1,0:T(8,128)(2,1)S(1)}, u32[]{:S(2)}, u32[]{:S(2)}) collective-permute-start(bf16[2,256,2048]{2,1,0:T(8,128)(2,1)} %refs_1_.7), channel_id=1, source_target_pairs={{0,1},{1,0},{2,3},{3,2},{4,5},{5,4},{6,7},{7,6},{8,9},{9,8},{10,11... | collective-permute-start | bytes 6291464 | tf_op jit(solution)/shard_map/ppermute | solution.py:757
  1.2 18.7 %collective-permute-start.3 = (bf16[2,256,2048]{2,1,0:T(8,128)(2,1)}, bf16[2,256,2048]{2,1,0:T(8,128)(2,1)}, u32[]{:S(2)}, u32[]{:S(2)}) collective-permute-start(bf16[2,256,2048]{2,1,0:T(8,128)(2,1)} %refs_17_.8), channel_id=1, source_target_pairs={{0,1},{1,0},{2,3},{3,2},{4,5},{5,4},{6,7},{7,6},{8,9},{9,8},{10,11... | collective-permute-start | bytes 6291464 | tf_op jit(solution)/shard_map/ppermute | solution.py:758
  3.9 9.2 %collective-permute-start.2 = (bf16[2,32,1024]{2,1,0:T(8,128)(2,1)}, bf16[2,32,1024]{2,1,0:T(8,128)(2,1)S(1)}, u32[]{:S(2)}, u32[]{:S(2)}) collective-permute-start(bf16[2,32,1024]{2,1,0:T(8,128)(2,1)} %get-tuple-element.50), channel_id=1, source_target_pairs={{1,3},{2,0},{3,5},{4,2},{5,7},{6,4},{7,9},{8,6},{9,11},{10,8},{11,... | collective-permute-start | bytes 393224 | tf_op jit(solution)/shard_map/ppermute | solution.py:756
  13.1 25.9 %collective-permute-start.10 = (bf16[128,2048]{1,0:T(8,128)(2,1)}, bf16[128,2048]{1,0:T(8,128)(2,1)S(1)}, u32[]{:S(2)}, u32[]{:S(2)}) collective-permute-start(bf16[128,2048]{1,0:T(8,128)(2,1)} %refs_17_.9), channel_id=1, source_target_pairs={{4,0},{8,4},{12,8},{14,12},{10,14},{6,10},{2,6},{0,2},{5,1},{9,5},... | collective-permute-start | bytes 1572872 | tf_op jit(solution)/shard_map/ppermute | solution.py:769
  16.1 24.2 %collective-permute-start.11 = (bf16[128,2048]{1,0:T(8,128)(2,1)}, bf16[128,2048]{1,0:T(8,128)(2,1)S(1)}, u32[]{:S(2)}, u32[]{:S(2)}) collective-permute-start(bf16[128,2048]{1,0:T(8,128)(2,1)} %refs_17_.9), channel_id=1, source_target_pairs={{0,4},{4,8},{8,12},{12,14},{14,10},{10,6},{6,2},{2,0},{1,5},{5,9},... | collective-permute-start | bytes 1572872 | tf_op jit(solution)/shard_map/ppermute | solution.py:766
  28.5 22.7 %collective-permute-start.4 = (bf16[128,2048]{1,0:T(8,128)(2,1)}, bf16[128,2048]{1,0:T(8,128)(2,1)S(1)}, u32[]{:S(2)}, u32[]{:S(2)}) collective-permute-start(bf16[128,2048]{1,0:T(8,128)(2,1)} %get-tuple-element.51), channel_id=1, source_target_pairs={{0,4},{4,8},{8,12},{12,14},{14,10},{10,6},{6,2},{2,0},{1,5},{5,9},... | collective-permute-start | bytes 1572872 | tf_op jit(solution)/shard_map/ppermute | solution.py:787
  30.6 20.6 %collective-permute-start.5 = (bf16[128,2048]{1,0:T(8,128)(2,1)}, bf16[128,2048]{1,0:T(8,128)(2,1)S(1)}, u32[]{:S(2)}, u32[]{:S(2)}) collective-permute-start(bf16[128,2048]{1,0:T(8,128)(2,1)} %get-tuple-element.55), channel_id=1, source_target_pairs={{4,0},{8,4},{12,8},{14,12},{10,14},{6,10},{2,6},{0,2},{5,1},{9,5},... | collective-permute-start | bytes 1572872 | tf_op jit(solution)/shard_map/ppermute | solution.py:787
  38.3 6.0 %collective-permute-start.6 = (bf16[2,16,2048]{2,1,0:T(8,128)(2,1)S(1)}, bf16[2,16,2048]{2,1,0:T(8,128)(2,1)S(1)}, u32[]{:S(2)}, u32[]{:S(2)}) collective-permute-start(bf16[2,16,2048]{2,1,0:T(8,128)(2,1)S(1)} %copy-done.24), channel_id=1, source_target_pairs={{1,2},{2,1},{3,4},{4,3},{5,6},{6,5},{7,8},{8,7},{9,10},{10,9},{11,... | collective-permute-start | bytes 393224 | tf_op jit(solution)/shard_map/ppermute | solution.py:799
  39.0 6.9 %collective-permute-start.7 = (bf16[2,16,2048]{2,1,0:T(8,128)(2,1)S(1)}, bf16[2,16,2048]{2,1,0:T(8,128)(2,1)S(1)}, u32[]{:S(2)}, u32[]{:S(2)}) collective-permute-start(bf16[2,16,2048]{2,1,0:T(8,128)(2,1)S(1)} %copy-done.24), channel_id=1, source_target_pairs={{1,3},{2,0},{3,5},{4,2},{5,7},{6,4},{7,9},{8,6},{9,11},{10,8},{11,... | collective-permute-start | bytes 393224 | tf_op jit(solution)/shard_map/ppermute | solution.py:800
  40.4 16.8 %collective-permute-start.13 = (bf16[64,2048]{1,0:T(8,128)(2,1)S(1)}, bf16[64,2048]{1,0:T(8,128)(2,1)S(1)}, u32[]{:S(2)}, u32[]{:S(2)}) collective-permute-start(bf16[64,2048]{1,0:T(8,128)(2,1)S(1)} %constant_dynamic-slice_fusion), channel_id=1, source_target_pairs={{0,4},{4,8},{8,12},{12,14},{14,10},{10,6},{6,2},{2,0},{1,5},{5,9},... | collective-permute-start | bytes 786440 | tf_op jit(solution)/shard_map/ppermute | solution.py:766
  51.3 42.1 %collective-permute-start.8 = (bf16[128,2048]{1,0:T(8,128)(2,1)S(1)}, bf16[128,2048]{1,0:T(8,128)(2,1)S(1)}, u32[]{:S(2)}, u32[]{:S(2)}) collective-permute-start(bf16[128,2048]{1,0:T(8,128)(2,1)S(1)} %add_convert_fusion.4), channel_id=1, source_target_pairs={{0,4},{4,8},{8,12},{12,14},{14,10},{10,6},{6,2},{2,0},{1,5},{5,9},... | collective-permute-start | bytes 1572872 | tf_op jit(solution)/shard_map/ppermute | solution.py:787
  56.2 37.3 %collective-permute-start.9 = (bf16[128,2048]{1,0:T(8,128)(2,1)S(1)}, bf16[128,2048]{1,0:T(8,128)(2,1)S(1)}, u32[]{:S(2)}, u32[]{:S(2)}) collective-permute-start(bf16[128,2048]{1,0:T(8,128)(2,1)S(1)} %add_convert_fusion.3), channel_id=1, source_target_pairs={{4,0},{8,4},{12,8},{14,12},{10,14},{6,10},{2,6},{0,2},{5,1},{9,5},... | collective-permute-start | bytes 1572872 | tf_op jit(solution)/shard_map/ppermute | solution.py:787
  56.3 17.9 %collective-permute-start.12 = (bf16[64,2048]{1,0:T(8,128)(2,1)S(1)}, bf16[64,2048]{1,0:T(8,128)(2,1)S(1)}, u32[]{:S(2)}, u32[]{:S(2)}) collective-permute-start(bf16[64,2048]{1,0:T(8,128)(2,1)S(1)} %constant_dynamic-slice_fusion.1), channel_id=1, source_target_pairs={{4,0},{8,4},{12,8},{14,12},{10,14},{6,10},{2,6},{0,2},{5,1},{9,5},... | collective-permute-start | bytes 786440 | tf_op jit(solution)/shard_map/ppermute | solution.py:769
  74.3 38.8 %collective-permute-start.14 = (bf16[128,2048]{1,0:T(8,128)(2,1)S(1)}, bf16[128,2048]{1,0:T(8,128)(2,1)S(1)}, u32[]{:S(2)}, u32[]{:S(2)}) collective-permute-start(bf16[128,2048]{1,0:T(8,128)(2,1)S(1)} %pad_maximum_fusion.1), channel_id=1, source_target_pairs={{0,16},{1,17},{2,18},{3,19},{4,20},{5,21},{6,22},{7,23},{8,24},{9,... | collective-permute-start | bytes 1572872 | tf_op jit(solution)/shard_map/ppermute | solution.py:832
  75.9 21.0 %collective-permute-start.19 = (bf16[64,2048]{1,0:T(8,128)(2,1)S(1)}, bf16[64,2048]{1,0:T(8,128)(2,1)S(1)}, u32[]{:S(2)}, u32[]{:S(2)}) collective-permute-start(bf16[64,2048]{1,0:T(8,128)(2,1)S(1)} %collective-permute-done.13.refs_18_), channel_id=1, source_target_pairs={{0,4},{4,8},{8,12},{12,14},{14,10},{10,6},{6,2},{2,0},{1,5},{5,9},... | collective-permute-start | bytes 786440 | tf_op jit(solution)/shard_map/ppermute | solution.py:766
  77.4 19.4 %collective-permute-start.18 = (bf16[64,2048]{1,0:T(8,128)(2,1)S(1)}, bf16[64,2048]{1,0:T(8,128)(2,1)S(1)}, u32[]{:S(2)}, u32[]{:S(2)}) collective-permute-start(bf16[64,2048]{1,0:T(8,128)(2,1)S(1)} %collective-permute-done.12.refs_21_), channel_id=1, source_target_pairs={{4,0},{8,4},{12,8},{14,12},{10,14},{6,10},{2,6},{0,2},{5,1},{9,5},... | collective-permute-start | bytes 786440 | tf_op jit(solution)/shard_map/ppermute | solution.py:769
  93.6 33.2 %collective-permute-start.16 = (bf16[128,2048]{1,0:T(8,128)(2,1)S(1)}, bf16[128,2048]{1,0:T(8,128)(2,1)S(1)}, u32[]{:S(2)}, u32[]{:S(2)}) collective-permute-start(bf16[128,2048]{1,0:T(8,128)(2,1)S(1)} %add_convert_fusion.2), channel_id=1, source_target_pairs={{0,4},{4,8},{8,12},{12,14},{14,10},{10,6},{6,2},{2,0},{1,5},{5,9},... | collective-permute-start | bytes 1572872 | tf_op jit(solution)/shard_map/ppermute | solution.py:787
  95.2 31.5 %collective-permute-start.17 = (bf16[128,2048]{1,0:T(8,128)(2,1)S(1)}, bf16[128,2048]{1,0:T(8,128)(2,1)S(1)}, u32[]{:S(2)}, u32[]{:S(2)}) collective-permute-start(bf16[128,2048]{1,0:T(8,128)(2,1)S(1)} %add_convert_fusion.1), channel_id=1, source_target_pairs={{4,0},{8,4},{12,8},{14,12},{10,14},{6,10},{2,6},{0,2},{5,1},{9,5},... | collective-permute-start | bytes 1572872 | tf_op jit(solution)/shard_map/ppermute | solution.py:787
  96.9 15.5 %collective-permute-start.20 = (bf16[64,2048]{1,0:T(8,128)(2,1)S(1)}, bf16[64,2048]{1,0:T(8,128)(2,1)S(1)}, u32[]{:S(2)}, u32[]{:S(2)}) collective-permute-start(bf16[64,2048]{1,0:T(8,128)(2,1)S(1)} %collective-permute-done.19.refs_21_), channel_id=1, source_target_pairs={{0,4},{4,8},{8,12},{12,14},{14,10},{10,6},{6,2},{2,0},{1,5},{5,9},... | collective-permute-start | bytes 786440 | tf_op jit(solution)/shard_map/ppermute | solution.py:766
  112.4 17.9 %collective-permute-start.21 = (bf16[192,2048]{1,0:T(8,128)(2,1)S(1)}, bf16[192,2048]{1,0:T(8,128)(2,1)S(1)}, u32[]{:S(2)}, u32[]{:S(2)}) collective-permute-start(bf16[192,2048]{1,0:T(8,128)(2,1)S(1)} %pad_maximum_fusion), channel_id=1, source_target_pairs={{0,16},{1,17},{2,18},{3,19},{4,20},{5,21},{6,22},{7,23},{8,24},{9,... | collective-permute-start | bytes 2359304 | tf_op jit(solution)/shard_map/ppermute | solution.py:832
  126.9 33.5 %collective-permute-start.23 = (bf16[128,2048]{1,0:T(8,128)(2,1)S(1)}, bf16[128,2048]{1,0:T(8,128)(2,1)S(1)}, u32[]{:S(2)}, u32[]{:S(2)}) collective-permute-start(bf16[128,2048]{1,0:T(8,128)(2,1)S(1)} %add_convert_fusion), channel_id=1, source_target_pairs={{0,4},{4,8},{8,12},{12,14},{14,10},{10,6},{6,2},{2,0},{1,5},{5,9},... | collective-permute-start | bytes 1572872 | tf_op jit(solution)/shard_map/ppermute | solution.py:862
  146.3 12.8 %all-to-all-start = ((f32[8,40,128]{2,1,0:T(8,128)}), f32[8,40,128]{2,1,0:T(8,128)S(1)}, u32[]{:S(2)}, u32[]{:S(2)}) async-start(f32[8,40,128]{2,1,0:T(8,128)} %deal.1), calls=%async_computation | async-start | bytes 327680 | tf_op jit(solution)/shard_map/all_to_all | solution.py:869
  152.9 8.6 %collective-permute-start.15 = (bf16[2,2,256,256]{3,2,1,0:T(8,128)(2,1)}, bf16[2,2,256,256]{3,2,1,0:T(8,128)(2,1)S(1)}, u32[]{:S(2)}, u32[]{:S(2)}) collective-permute-start(bf16[2,2,256,256]{3,2,1,0:T(8,128)(2,1)} %get-tuple-element.77), channel_id=1, source_target_pairs={{0,1},{1,0},{2,3},{3,2},{4,5},{5,4},{6,7},{7,6},{8,9},{9,8},{10,11... | collective-permute-start | bytes 1572872 | tf_op jit(solution)/shard_map/ppermute | solution.py:861
  153.0 8.5 %collective-permute-start.22 = (bf16[2,2,256,256]{3,2,1,0:T(8,128)(2,1)}, bf16[2,2,256,256]{3,2,1,0:T(8,128)(2,1)S(1)}, u32[]{:S(2)}, u32[]{:S(2)}) collective-permute-start(bf16[2,2,256,256]{3,2,1,0:T(8,128)(2,1)} %get-tuple-element.90), channel_id=1, source_target_pairs={{0,1},{1,0},{2,3},{3,2},{4,5},{5,4},{6,7},{7,6},{8,9},{9,8},{10,11... | collective-permute-start | bytes 1572872 | tf_op jit(solution)/shard_map/ppermute | solution.py:861
  (26 other events, 257.3 us)
where the time goes:
time: 167 us
  Pallas kernels  69.1 us (41%)
  waiting for transfers between devices  49.4 us (30%)
  starting transfers between devices  34.9 us (21%)
  local copies, waits for them, and re-layouts  8.88 us (5%)
  other arithmetic  2.49 us (1%)
  between operations  1.8 us (1%)
    pallas_call x4, Pallas kernels, conv_call(): pl.pallas_call(functools.partial(conv_body, plan), grid_spec=pltpu.Prefet...  30.3 us
    pallas_call x2, Pallas kernels, back_call(): pl.pallas_call(functools.partial(back_body, plan, steps, sources), grid_s...  25.7 us
    ppermute x3, waiting for transfers between devices, weight_round(): going[1] = lax.ppermute(going[1], 'shard', backward)  17.1 us
    ppermute x4, waiting for transfers between devices, weight_round(): going[0] = lax.ppermute(going[0], 'shard', forward)  14.9 us
    ppermute x3, starting transfers between devices, sum_round(): lax.ppermute(send[0], 'shard', forward)  8.32 us
    ppermute x1, waiting for transfers between devices, ring_shards(): xb = lax.ppermute(x_far, 'shard', plan.edges_like())  7.89 us
    ppermute x4, starting transfers between devices, weight_round(): going[0] = lax.ppermute(going[0], 'shard', forward)  7.57 us
    all_to_all x1, waiting for transfers between devices, ring_shards(): lax.all_to_all(dealt, 'shard', 0, 0, axis_index_groups=groups)  5.66 us
  transfers between devices with their start and end apart: 25, of which 6 were waited for; matrix products, arithmetic and copies ran while one was open for 4% of the time, Pallas kernels for 39%

commit v1 on v0

--- a/solution.py
+++ b/solution.py
@@ -760,7 +760,10 @@
     halved = plan.weight_parts == 2
     piece = LANES // 2
     around = {}
-    going = [after(proj_weight, xa, xb)] * 2
+    going = [proj_weight] * 2
+    if halved:
+        going = [lax.dynamic_slice_in_dim(proj_weight, group * piece, piece, 0)] * 2
+    xa, xb, taps, info = lax.optimization_barrier((xa, xb, taps, info))
 
     def weight_round(step):
         going[0] = lax.ppermute(going[0], "shard", forward)
@@ -793,23 +796,24 @@
             for product, value, kind in zip(own, received, kinds)
         ]
 
+    def wait_for(value):
+        going[:] = lax.optimization_barrier((*going, value))[:2]
+
     weight_round(1)
     conv_step(0, info)
     g_edge = after(g_edge, products[0][0])
     ga = lax.ppermute(g_edge, "shard", plan.edges())
     gb = lax.ppermute(g_edge, "shard", plan.edges_like())
+    wait_for(products[0][0])
+    weight_round(2)
     conv_step(1, after(info, products[0][0]))
-    going = list(lax.optimization_barrier((*going, products[1][0]))[:2])
-    if halved:
-        going = [lax.dynamic_slice_in_dim(w, group * piece, piece, 0) for w in going]
-    weight_round(2)
+    wait_for(products[1][0])
+    weight_round(3)
     mg = assemble_call(plan, after(info, products[1][0]), grad_out, mgp, ga, gb)
+    wait_for(mg)
+    weight_round(4)
     send = sum_round(1, products[0], mg)
-    going = list(lax.optimization_barrier((*going, mg))[:2])
-    weight_round(3)
     conv_step(2, after(info, products[1][0], *send, mg))
-    going = list(lax.optimization_barrier((*going, products[2][0]))[:2])
-    weight_round(4)
     conv_step(3, after(info, products[2][0]))
     send = sum_round(2, send, products[3][0])
 
@@ -823,8 +827,8 @@
     swap = [
         (g * plan.count + s, (1 - g) * plan.count + s) for g in range(2) for s in range(plan.count)
     ]
-    for n, distances in enumerate([[1, -1], [2, -2], [3, -3, 4]]):
-        if n == 0 or not halved:
+    for distances in ([1, -1], [2, -2], [3, -3, 4]):
+        if not halved:
             for d in distances:
                 source[d] = [(keep(around[d]), None, 0, LANES)]
             continue
@@ -861,13 +865,11 @@
         pieces += [own, lax.ppermute(given, "shard", plan.partners())]
     recv_f = after(lax.ppermute(send[0], "shard", forward), stats[-1])
     proj_grad = (send[1] + recv_f.astype(jnp.float32)) * scale
-    full = place_call(plan, calls, info, pieces)
-
     dealt = deal_call(plan, calls, info, stats)
     groups = [[CORES * p + c for p in range(plan.chips)] for c in range(CORES)]
-    summed = jnp.sum(
-        lax.all_to_all(dealt, "shard", 0, 0, axis_index_groups=groups), axis=0
-    ) * scale
+    shares = lax.all_to_all(dealt, "shard", 0, 0, axis_index_groups=groups)
+    full = place_call(plan, calls, after(info, dealt), pieces)
+    summed = jnp.sum(after(shares, full, proj_grad), axis=0) * scale
     return (
         full, proj_grad, summed[: plan.taps], summed[plan.tap_rows : plan.tap_rows + 2]
     )

time: 167 us -> 158 us (0.946)
  waiting for transfers between devices: 49.4 us -> 38.7 us
    ppermute x3, waiting for transfers between devices: 17.1 us -> 6.15 us  [weight_round(): going[1] = lax.ppermute(going[1], 'shard', backward)]
    ppermute x4, waiting for transfers between devices: 14.9 us -> 22.1 us  [weight_round(): going[0] = lax.ppermute(going[0], 'shard', forward)]
    all_to_all x1, waiting for transfers between devices: 5.66 us -> 1.93 us  [ring_shards(): shares = lax.all_to_all(dealt, 'shard', 0, 0, axis_index_groups=groups)]
    ppermute x3, starting transfers between devices: 8.32 us -> 6.1 us  [sum_round(): lax.ppermute(send[0], 'shard', forward)]
    ppermute x2 -> x3, starting transfers between devices: 2.25 us -> 3.79 us  [ring_shards(): lax.ppermute(jnp.concatenate([around[d] for d in distances], 0), ('groups...]
    unnamed x50 -> x56, local copies, waits for them, and re-layouts: 5.39 us -> 6.52 us
  transfers between devices with their start and end apart: 25 -> 26, of which waited for: 6 -> 7; matrix products, arithmetic and copies ran while one was open for 4% -> 3% of each run, Pallas kernels for 39% -> 39%
where the time goes in v1:
time: 158 us; the launch traced here: 157 us
  Pallas kernels  68.9 us (44%)
  waiting for transfers between devices  38.7 us (24%)
  starting transfers between devices  35.6 us (23%)
  local copies, waits for them, and re-layouts  9.1 us (6%)
  other arithmetic  3.35 us (2%)
  between operations  1.85 us (1%)
    pallas_call x4, Pallas kernels, conv_call(): pl.pallas_call(functools.partial(conv_body, plan), grid_spec=pltpu.Prefet...  30.3 us
    pallas_call x2, Pallas kernels, back_call(): pl.pallas_call(functools.partial(back_body, plan, steps, sources), grid_s...  25.5 us
    ppermute x4, waiting for transfers between devices, weight_round(): going[0] = lax.ppermute(going[0], 'shard', forward)  22.1 us
    ppermute x4, starting transfers between devices, weight_round(): going[0] = lax.ppermute(going[0], 'shard', forward)  8.32 us
    unnamed x56, local copies, waits for them, and re-layouts  6.52 us
    ppermute x1, waiting for transfers between devices, ring_shards(): xb = lax.ppermute(x_far, 'shard', plan.edges_like())  6.44 us
    ppermute x3, waiting for transfers between devices, weight_round(): going[1] = lax.ppermute(going[1], 'shard', backward)  6.15 us
    ppermute x3, starting transfers between devices, sum_round(): lax.ppermute(send[0], 'shard', forward)  6.1 us
  transfers between devices with their start and end apart: 26, of which 7 were waited for; matrix products, arithmetic and copies ran while one was open for 3% of the time, Pallas kernels for 39%

profile of v1, /device:TPU:0, one launch (start us, length us, event | category | flops | bytes accessed | tf_op | source)
XLA Modules:
  0.0 157.5 jit_solution(2686177561004335512)
XLA Ops:
  1.3 1.9 %edge.1 = (bf16[2,32,1024]{2,1,0:T(8,128)(2,1)}, bf16[2,32,1024]{2,1,0:T(8,128)(2,1)}, bf16[2,16,2048]{2,1,0:T(8,128)(2,1)}) custom-call(bf16[2,256,2048]{2,1,0:T(8,128)(2,1)} %refs_1_.7, bf16[2,256,2048]{2,1,0:T(8,128)(2,1)} %refs_1_.7, bf16[2,256,2048]{2,1,0:T(8,128)(2,1)} %refs_17_.8, bf16[2,256,2048]{2,1,0:T(8,128)(2,1)} %refs_17_.8), custom_call_target="tpu_custom_call" | custom-call | bytes 3600000 | tf_op jit(solution)/shard_map/edge/pallas_call | solution.py:674
  6.7 6.4 %collective-permute-done.1.refs_6_.refs_7_ = bf16[2,32,1024]{2,1,0:T(8,128)(2,1)S(1)} collective-permute-done((bf16[2,32,1024]{2,1,0:T(8,128)(2,1)}, bf16[2,32,1024]{2,1,0:T(8,128)(2,1)S(1)}, u32[]{:S(2)}, u32[]{:S(2)}) %collective-permute-start.1) | collective-permute-done | bytes 131104 | tf_op jit(solution)/shard_map/ppermute | solution.py:756
  14.5 7.4 %conv.4 = (f32[2,544,256]{2,1,0:T(8,128)}, bf16[2,640,256]{2,1,0:T(8,128)(2,1)}, bf16[128,2048]{1,0:T(8,128)(2,1)}, bf16[128,2048]{1,0:T(8,128)(2,1)}) custom-call(s32[13]{0:T(128)} %concatenate.12.info, bf16[2,256,2048]{2,1,0:T(8,128)(2,1)} %refs_1_.7, bf16[2,256,2048]{2,1,0:T(8,128)(2,1)} %refs_1_.7, bf16[2,256,2048]{2,1,0:T(8,128)(2,1)} %copy-done, ...), custom_call_target="tpu_custom_call" | custom-call | bytes 21600000 | tf_op jit(solution)/shard_map/conv/pallas_call | solution.py:350
  21.9 4.6 %collective-permute-start.4 = (bf16[128,2048]{1,0:T(8,128)(2,1)}, bf16[128,2048]{1,0:T(8,128)(2,1)S(1)}, u32[]{:S(2)}, u32[]{:S(2)}) collective-permute-start(bf16[128,2048]{1,0:T(8,128)(2,1)} %get-tuple-element.60), channel_id=1, source_target_pairs={{0,4},{4,8},{8,12},{12,14},{14,10},{10,6},{6,2},{2,0},{1,5},{5,9},... | collective-permute-start | bytes 1572872 | tf_op jit(solution)/shard_map/ppermute | solution.py:790
  28.5 4.2 %collective-permute-start.11 = (bf16[64,2048]{1,0:T(8,128)(2,1)S(1)}, bf16[64,2048]{1,0:T(8,128)(2,1)S(1)}, u32[]{:S(2)}, u32[]{:S(2)}) collective-permute-start(bf16[64,2048]{1,0:T(8,128)(2,1)S(1)} %constant_dynamic-slice_fusion), channel_id=1, source_target_pairs={{0,4},{4,8},{8,12},{12,14},{14,10},{10,6},{6,2},{2,0},{1,5},{5,9},... | collective-permute-start | bytes 786440 | tf_op jit(solution)/shard_map/ppermute | solution.py:769
  32.7 7.6 %conv.5 = (f32[2,544,256]{2,1,0:T(8,128)}, bf16[2,640,256]{2,1,0:T(8,128)(2,1)}, f32[128,2048]{1,0:T(8,128)}, f32[128,2048]{1,0:T(8,128)}) custom-call(s32[13]{0:T(128)} %concatenate.12.info, bf16[2,256,2048]{2,1,0:T(8,128)(2,1)} %refs_1_.7, bf16[2,256,2048]{2,1,0:T(8,128)(2,1)} %refs_1_.7, bf16[2,256,2048]{2,1,0:T(8,128)(2,1)} %copy-done, ...), custom_call_target="tpu_custom_call" | custom-call | bytes 21600000 | tf_op jit(solution)/shard_map/conv/pallas_call | solution.py:350
  40.3 3.8 %collective-permute-start.10 = (bf16[64,2048]{1,0:T(8,128)(2,1)S(1)}, bf16[64,2048]{1,0:T(8,128)(2,1)S(1)}, u32[]{:S(2)}, u32[]{:S(2)}) collective-permute-start(bf16[64,2048]{1,0:T(8,128)(2,1)S(1)} %constant_dynamic-slice_fusion), channel_id=1, source_target_pairs={{4,0},{8,4},{12,8},{14,12},{10,14},{6,10},{2,6},{0,2},{5,1},{9,5},... | collective-permute-start | bytes 786440 | tf_op jit(solution)/shard_map/ppermute | solution.py:772
  44.7 4.7 %assemble.1.refs_0_ = bf16[2,544,2048]{2,1,0:T(8,128)(2,1)} custom-call(s32[13]{0:T(128)} %concatenate.12.info, bf16[2,256,2048]{2,1,0:T(8,128)(2,1)} %refs_17_.8, bf16[2,256,2048]{2,1,0:T(8,128)(2,1)} %collective-permute-done.3.refs_18_.other_ref, bf16[2,16,2048]{2,1,0:T(8,128)(2,1)} %copy-done.23, bf16[2,16,2048]{2,1,0:T(8,128)(2,1)} %copy-done.24), custom_call_target="tpu_custom_call" | custom-call | bytes 18000000 | tf_op jit(solution)/shard_map/assemble/pallas_call | solution.py:719
  54.0 1.6 %collective-permute-start.12 = (bf16[128,2048]{1,0:T(8,128)(2,1)S(1)}, bf16[128,2048]{1,0:T(8,128)(2,1)S(1)}, u32[]{:S(2)}, u32[]{:S(2)}) collective-permute-start(bf16[128,2048]{1,0:T(8,128)(2,1)S(1)} %pad_maximum_fusion.1), channel_id=1, source_target_pairs={{0,16},{1,17},{2,18},{3,19},{4,20},{5,21},{6,22},{7,23},{8,24},{9,... | collective-permute-start | bytes 1572872 | tf_op jit(solution)/shard_map/ppermute | solution.py:836
  55.5 13.3 %collective-permute-done.14.refs_18_ = bf16[64,2048]{1,0:T(8,128)(2,1)S(1)} collective-permute-done((bf16[64,2048]{1,0:T(8,128)(2,1)S(1)}, bf16[64,2048]{1,0:T(8,128)(2,1)S(1)}, u32[]{:S(2)}, u32[]{:S(2)}) %collective-permute-start.14) | collective-permute-done | bytes 262176 | tf_op jit(solution)/shard_map/ppermute | solution.py:769
  69.8 1.6 %collective-permute-start.15 = (bf16[128,2048]{1,0:T(8,128)(2,1)S(1)}, bf16[128,2048]{1,0:T(8,128)(2,1)S(1)}, u32[]{:S(2)}, u32[]{:S(2)}) collective-permute-start(bf16[128,2048]{1,0:T(8,128)(2,1)S(1)} %pad_maximum_fusion.2), channel_id=1, source_target_pairs={{0,16},{1,17},{2,18},{3,19},{4,20},{5,21},{6,22},{7,23},{8,24},{9,... | collective-permute-start | bytes 1572872 | tf_op jit(solution)/shard_map/ppermute | solution.py:836
  72.8 7.6 %conv.6 = (f32[2,544,256]{2,1,0:T(8,128)}, bf16[2,640,256]{2,1,0:T(8,128)(2,1)}, f32[128,2048]{1,0:T(8,128)}, f32[128,2048]{1,0:T(8,128)}) custom-call(s32[13]{0:T(128)} %concatenate.12.info, bf16[2,256,2048]{2,1,0:T(8,128)(2,1)} %refs_1_.7, bf16[2,256,2048]{2,1,0:T(8,128)(2,1)} %refs_1_.7, bf16[2,256,2048]{2,1,0:T(8,128)(2,1)} %copy-done, ...), custom_call_target="tpu_custom_call" | custom-call | bytes 21600000 | tf_op jit(solution)/shard_map/conv/pallas_call | solution.py:350
  80.5 7.8 %conv.7 = (f32[2,544,256]{2,1,0:T(8,128)}, bf16[2,640,256]{2,1,0:T(8,128)(2,1)}, f32[128,2048]{1,0:T(8,128)}, f32[128,2048]{1,0:T(8,128)}) custom-call(s32[13]{0:T(128)} %concatenate.12.info, bf16[2,256,2048]{2,1,0:T(8,128)(2,1)} %refs_1_.7, bf16[2,256,2048]{2,1,0:T(8,128)(2,1)} %refs_1_.7, bf16[2,256,2048]{2,1,0:T(8,128)(2,1)} %copy-done, ...), custom_call_target="tpu_custom_call" | custom-call | bytes 21600000 | tf_op jit(solution)/shard_map/conv/pallas_call | solution.py:350
  89.1 1.5 collective-permute-start.16
  92.1 5.3 %collective-permute-done.18.refs_20_ = bf16[64,2048]{1,0:T(8,128)(2,1)S(1)} collective-permute-done((bf16[64,2048]{1,0:T(8,128)(2,1)S(1)}, bf16[64,2048]{1,0:T(8,128)(2,1)S(1)}, u32[]{:S(2)}, u32[]{:S(2)}) %collective-permute-start.18) | collective-permute-done | bytes 262176 | tf_op jit(solution)/shard_map/ppermute | solution.py:772
  97.4 1.6 %collective-permute-start.20 = (bf16[64,2048]{1,0:T(8,128)(2,1)S(1)}, bf16[64,2048]{1,0:T(8,128)(2,1)S(1)}, u32[]{:S(2)}, u32[]{:S(2)}) collective-permute-start(bf16[64,2048]{1,0:T(8,128)(2,1)S(1)} %collective-permute-done.19.refs_21_), channel_id=1, source_target_pairs={{0,4},{4,8},{8,12},{12,14},{14,10},{10,6},{6,2},{2,0},{1,5},{5,9},... | collective-permute-start | bytes 786440 | tf_op jit(solution)/shard_map/ppermute | solution.py:769
  99.0 8.8 %collective-permute-done.20.refs_22_ = bf16[64,2048]{1,0:T(8,128)(2,1)S(1)} collective-permute-done((bf16[64,2048]{1,0:T(8,128)(2,1)S(1)}, bf16[64,2048]{1,0:T(8,128)(2,1)S(1)}, u32[]{:S(2)}, u32[]{:S(2)}) %collective-permute-start.20) | collective-permute-done | bytes 262176 | tf_op jit(solution)/shard_map/ppermute | solution.py:769
  109.4 12.8 %back.2 = (bf16[2,2,256,256]{3,2,1,0:T(8,128)(2,1)}, bf16[2,2,256,256]{3,2,1,0:T(8,128)(2,1)}, f32[2,40,256]{2,1,0:T(8,128)}) custom-call(s32[13]{0:T(128)} %concatenate.12.info, bf16[2,544,2048]{2,1,0:T(8,128)(2,1)} %assemble.1.refs_0_, f32[32,2048]{1,0:T(8,128)} %pad.4.refs_8_.refs_9_.refs_1_.refs_2_.refs_3_.refs_4_, ...), custom_call_target="tpu_custom_call" | custom-call | bytes 43200000 | tf_op jit(solution)/shard_map/back/pallas_call | solution.py:546
  123.7 2.0 %collective-permute-done.21.refs_19_ = bf16[192,2048]{1,0:T(8,128)(2,1)S(1)} collective-permute-done((bf16[192,2048]{1,0:T(8,128)(2,1)S(1)}, bf16[192,2048]{1,0:T(8,128)(2,1)S(1)}, u32[]{:S(2)}, u32[]{:S(2)}) %collective-permute-start.21) | collective-permute-done | bytes 786464 | tf_op jit(solution)/shard_map/ppermute | solution.py:836
  126.5 12.7 %back.3 = (bf16[2,2,256,256]{3,2,1,0:T(8,128)(2,1)}, bf16[2,2,256,256]{3,2,1,0:T(8,128)(2,1)}, f32[2,40,256]{2,1,0:T(8,128)}) custom-call(s32[13]{0:T(128)} %concatenate.12.info, bf16[2,544,2048]{2,1,0:T(8,128)(2,1)} %assemble.1.refs_0_, f32[32,2048]{1,0:T(8,128)} %pad.4.refs_8_.refs_9_.refs_1_.refs_2_.refs_3_.refs_4_, ...), custom_call_target="tpu_custom_call" | custom-call | bytes 43200000 | tf_op jit(solution)/shard_map/back/pallas_call | solution.py:546
  140.6 2.3 %deal.1 = f32[8,40,128]{2,1,0:T(8,128)} custom-call(s32[13]{0:T(128)} %concatenate.12.info, f32[2,40,256]{2,1,0:T(8,128)} %get-tuple-element.84.refs_0_, f32[2,40,256]{2,1,0:T(8,128)} %get-tuple-element.97.refs_1_), custom_call_target="tpu_custom_call" | custom-call | bytes 3600000 | tf_op jit(solution)/shard_map/deal/pallas_call | solution.py:637
  142.9 5.2 %all-to-all-start = ((f32[8,40,128]{2,1,0:T(8,128)}), f32[8,40,128]{2,1,0:T(8,128)S(1)}, u32[]{:S(2)}, u32[]{:S(2)}) async-start(f32[8,40,128]{2,1,0:T(8,128)} %deal.1), calls=%async_computation | async-start | bytes 327680 | tf_op jit(solution)/shard_map/all_to_all | solution.py:870
  149.1 4.1 %place.1 = bf16[2,256,2048]{2,1,0:T(8,128)(2,1)} custom-call(s32[13]{0:T(128)} %concatenate.12.info, bf16[2,2,256,256]{3,2,1,0:T(8,128)(2,1)} %get-tuple-element.86.refs_0_, bf16[2,2,256,256]{3,2,1,0:T(8,128)(2,1)} %copy-done.20, bf16[2,2,256,256]{3,2,1,0:T(8,128)(2,1)} %get-tuple-element.100.refs_2_, bf16[2,2,256,256]{3,2,1,0:T(8,128)(2,1)} %copy-done.21), custom_call_target="tpu_custom_call" | custom-call | bytes 10800000 | tf_op jit(solution)/shard_map/place/pallas_call | solution.py:611
  154.4 1.9 %all-to-all-done = f32[8,40,128]{2,1,0:T(8,128)S(1)} async-done(((f32[8,40,128]{2,1,0:T(8,128)}), f32[8,40,128]{2,1,0:T(8,128)S(1)}, u32[]{:S(2)}, u32[]{:S(2)}) %all-to-all-start) | async-done | bytes 163872 | tf_op jit(solution)/shard_map/all_to_all | solution.py:870
  (113 shorter events, 25.0 us)
Async XLA Ops:
  0.7 12.4 %collective-permute-start.2 = (bf16[2,256,2048]{2,1,0:T(8,128)(2,1)}, bf16[2,256,2048]{2,1,0:T(8,128)(2,1)S(1)}, u32[]{:S(2)}, u32[]{:S(2)}) collective-permute-start(bf16[2,256,2048]{2,1,0:T(8,128)(2,1)} %refs_1_.7), channel_id=1, source_target_pairs={{0,1},{1,0},{2,3},{3,2},{4,5},{5,4},{6,7},{7,6},{8,9},{9,8},{10,11... | collective-permute-start | bytes 6291464 | tf_op jit(solution)/shard_map/ppermute | solution.py:757
  1.2 11.9 %collective-permute-start.3 = (bf16[2,256,2048]{2,1,0:T(8,128)(2,1)}, bf16[2,256,2048]{2,1,0:T(8,128)(2,1)}, u32[]{:S(2)}, u32[]{:S(2)}) collective-permute-start(bf16[2,256,2048]{2,1,0:T(8,128)(2,1)} %refs_17_.8), channel_id=1, source_target_pairs={{0,1},{1,0},{2,3},{3,2},{4,5},{5,4},{6,7},{7,6},{8,9},{9,8},{10,11... | collective-permute-start | bytes 6291464 | tf_op jit(solution)/shard_map/ppermute | solution.py:758
  3.9 9.2 %collective-permute-start.1 = (bf16[2,32,1024]{2,1,0:T(8,128)(2,1)}, bf16[2,32,1024]{2,1,0:T(8,128)(2,1)S(1)}, u32[]{:S(2)}, u32[]{:S(2)}) collective-permute-start(bf16[2,32,1024]{2,1,0:T(8,128)(2,1)} %get-tuple-element.55), channel_id=1, source_target_pairs={{1,3},{2,0},{3,5},{4,2},{5,7},{6,4},{7,9},{8,6},{9,11},{10,8},{11,... | collective-permute-start | bytes 393224 | tf_op jit(solution)/shard_map/ppermute | solution.py:756
  21.9 27.5 %collective-permute-start.4 = (bf16[128,2048]{1,0:T(8,128)(2,1)}, bf16[128,2048]{1,0:T(8,128)(2,1)S(1)}, u32[]{:S(2)}, u32[]{:S(2)}) collective-permute-start(bf16[128,2048]{1,0:T(8,128)(2,1)} %get-tuple-element.60), channel_id=1, source_target_pairs={{0,4},{4,8},{8,12},{12,14},{14,10},{10,6},{6,2},{2,0},{1,5},{5,9},... | collective-permute-start | bytes 1572872 | tf_op jit(solution)/shard_map/ppermute | solution.py:790
  26.5 23.0 %collective-permute-start.5 = (bf16[128,2048]{1,0:T(8,128)(2,1)}, bf16[128,2048]{1,0:T(8,128)(2,1)S(1)}, u32[]{:S(2)}, u32[]{:S(2)}) collective-permute-start(bf16[128,2048]{1,0:T(8,128)(2,1)} %get-tuple-element.64), channel_id=1, source_target_pairs={{4,0},{8,4},{12,8},{14,12},{10,14},{6,10},{2,6},{0,2},{5,1},{9,5},... | collective-permute-start | bytes 1572872 | tf_op jit(solution)/shard_map/ppermute | solution.py:790
  26.5 13.8 %collective-permute-start.6 = (bf16[2,16,2048]{2,1,0:T(8,128)(2,1)S(1)}, bf16[2,16,2048]{2,1,0:T(8,128)(2,1)S(1)}, u32[]{:S(2)}, u32[]{:S(2)}) collective-permute-start(bf16[2,16,2048]{2,1,0:T(8,128)(2,1)S(1)} %copy-done.27), channel_id=1, source_target_pairs={{1,2},{2,1},{3,4},{4,3},{5,6},{6,5},{7,8},{8,7},{9,10},{10,9},{11,... | collective-permute-start | bytes 393224 | tf_op jit(solution)/shard_map/ppermute | solution.py:805
  27.1 16.9 %collective-permute-start.7 = (bf16[2,16,2048]{2,1,0:T(8,128)(2,1)S(1)}, bf16[2,16,2048]{2,1,0:T(8,128)(2,1)S(1)}, u32[]{:S(2)}, u32[]{:S(2)}) collective-permute-start(bf16[2,16,2048]{2,1,0:T(8,128)(2,1)S(1)} %copy-done.27), channel_id=1, source_target_pairs={{1,3},{2,0},{3,5},{4,2},{5,7},{6,4},{7,9},{8,6},{9,11},{10,8},{11,... | collective-permute-start | bytes 393224 | tf_op jit(solution)/shard_map/ppermute | solution.py:806
  28.5 23.3 %collective-permute-start.11 = (bf16[64,2048]{1,0:T(8,128)(2,1)S(1)}, bf16[64,2048]{1,0:T(8,128)(2,1)S(1)}, u32[]{:S(2)}, u32[]{:S(2)}) collective-permute-start(bf16[64,2048]{1,0:T(8,128)(2,1)S(1)} %constant_dynamic-slice_fusion), channel_id=1, source_target_pairs={{0,4},{4,8},{8,12},{12,14},{14,10},{10,6},{6,2},{2,0},{1,5},{5,9},... | collective-permute-start | bytes 786440 | tf_op jit(solution)/shard_map/ppermute | solution.py:769
  40.3 11.5 %collective-permute-start.10 = (bf16[64,2048]{1,0:T(8,128)(2,1)S(1)}, bf16[64,2048]{1,0:T(8,128)(2,1)S(1)}, u32[]{:S(2)}, u32[]{:S(2)}) collective-permute-start(bf16[64,2048]{1,0:T(8,128)(2,1)S(1)} %constant_dynamic-slice_fusion), channel_id=1, source_target_pairs={{4,0},{8,4},{12,8},{14,12},{10,14},{6,10},{2,6},{0,2},{5,1},{9,5},... | collective-permute-start | bytes 786440 | tf_op jit(solution)/shard_map/ppermute | solution.py:772
  49.6 38.7 %collective-permute-start.8 = (bf16[128,2048]{1,0:T(8,128)(2,1)S(1)}, bf16[128,2048]{1,0:T(8,128)(2,1)S(1)}, u32[]{:S(2)}, u32[]{:S(2)}) collective-permute-start(bf16[128,2048]{1,0:T(8,128)(2,1)S(1)} %add_convert_fusion.4), channel_id=1, source_target_pairs={{0,4},{4,8},{8,12},{12,14},{14,10},{10,6},{6,2},{2,0},{1,5},{5,9},... | collective-permute-start | bytes 1572872 | tf_op jit(solution)/shard_map/ppermute | solution.py:790
  50.8 38.2 %collective-permute-start.9 = (bf16[128,2048]{1,0:T(8,128)(2,1)S(1)}, bf16[128,2048]{1,0:T(8,128)(2,1)S(1)}, u32[]{:S(2)}, u32[]{:S(2)}) collective-permute-start(bf16[128,2048]{1,0:T(8,128)(2,1)S(1)} %add_convert_fusion.3), channel_id=1, source_target_pairs={{4,0},{8,4},{12,8},{14,12},{10,14},{6,10},{2,6},{0,2},{5,1},{9,5},... | collective-permute-start | bytes 1572872 | tf_op jit(solution)/shard_map/ppermute | solution.py:790
  51.8 17.1 %collective-permute-start.14 = (bf16[64,2048]{1,0:T(8,128)(2,1)S(1)}, bf16[64,2048]{1,0:T(8,128)(2,1)S(1)}, u32[]{:S(2)}, u32[]{:S(2)}) collective-permute-start(bf16[64,2048]{1,0:T(8,128)(2,1)S(1)} %collective-permute-done.11.refs_20_), channel_id=1, source_target_pairs={{0,4},{4,8},{8,12},{12,14},{14,10},{10,6},{6,2},{2,0},{1,5},{5,9},... | collective-permute-start | bytes 786440 | tf_op jit(solution)/shard_map/ppermute | solution.py:769
  52.9 16.8 %collective-permute-start.13 = (bf16[64,2048]{1,0:T(8,128)(2,1)S(1)}, bf16[64,2048]{1,0:T(8,128)(2,1)S(1)}, u32[]{:S(2)}, u32[]{:S(2)}) collective-permute-start(bf16[64,2048]{1,0:T(8,128)(2,1)S(1)} %collective-permute-done.10.refs_19_), channel_id=1, source_target_pairs={{4,0},{8,4},{12,8},{14,12},{10,14},{6,10},{2,6},{0,2},{5,1},{9,5},... | collective-permute-start | bytes 786440 | tf_op jit(solution)/shard_map/ppermute | solution.py:772
  54.0 54.5 %collective-permute-start.12 = (bf16[128,2048]{1,0:T(8,128)(2,1)S(1)}, bf16[128,2048]{1,0:T(8,128)(2,1)S(1)}, u32[]{:S(2)}, u32[]{:S(2)}) collective-permute-start(bf16[128,2048]{1,0:T(8,128)(2,1)S(1)} %pad_maximum_fusion.1), channel_id=1, source_target_pairs={{0,16},{1,17},{2,18},{3,19},{4,20},{5,21},{6,22},{7,23},{8,24},{9,... | collective-permute-start | bytes 1572872 | tf_op jit(solution)/shard_map/ppermute | solution.py:836
  69.8 38.7 %collective-permute-start.15 = (bf16[128,2048]{1,0:T(8,128)(2,1)S(1)}, bf16[128,2048]{1,0:T(8,128)(2,1)S(1)}, u32[]{:S(2)}, u32[]{:S(2)}) collective-permute-start(bf16[128,2048]{1,0:T(8,128)(2,1)S(1)} %pad_maximum_fusion.2), channel_id=1, source_target_pairs={{0,16},{1,17},{2,18},{3,19},{4,20},{5,21},{6,22},{7,23},{8,24},{9,... | collective-permute-start | bytes 1572872 | tf_op jit(solution)/shard_map/ppermute | solution.py:836
  71.4 20.1 %collective-permute-start.19 = (bf16[64,2048]{1,0:T(8,128)(2,1)S(1)}, bf16[64,2048]{1,0:T(8,128)(2,1)S(1)}, u32[]{:S(2)}, u32[]{:S(2)}) collective-permute-start(bf16[64,2048]{1,0:T(8,128)(2,1)S(1)} %collective-permute-done.14.refs_18_), channel_id=1, source_target_pairs={{0,4},{4,8},{8,12},{12,14},{14,10},{10,6},{6,2},{2,0},{1,5},{5,9},... | collective-permute-start | bytes 786440 | tf_op jit(solution)/shard_map/ppermute | solution.py:769
  88.3 9.1 %collective-permute-start.18 = (bf16[64,2048]{1,0:T(8,128)(2,1)S(1)}, bf16[64,2048]{1,0:T(8,128)(2,1)S(1)}, u32[]{:S(2)}, u32[]{:S(2)}) collective-permute-start(bf16[64,2048]{1,0:T(8,128)(2,1)S(1)} %collective-permute-done.13.refs_22_), channel_id=1, source_target_pairs={{4,0},{8,4},{12,8},{14,12},{10,14},{6,10},{2,6},{0,2},{5,1},{9,5},... | collective-permute-start | bytes 786440 | tf_op jit(solution)/shard_map/ppermute | solution.py:772
  89.1 33.3 %collective-permute-start.16 = (bf16[128,2048]{1,0:T(8,128)(2,1)S(1)}, bf16[128,2048]{1,0:T(8,128)(2,1)S(1)}, u32[]{:S(2)}, u32[]{:S(2)}) collective-permute-start(bf16[128,2048]{1,0:T(8,128)(2,1)S(1)} %add_convert_fusion.2), channel_id=1, source_target_pairs={{0,4},{4,8},{8,12},{12,14},{14,10},{10,6},{6,2},{2,0},{1,5},{5,9},... | collective-permute-start | bytes 1572872 | tf_op jit(solution)/shard_map/ppermute | solution.py:790
  91.4 31.0 %collective-permute-start.17 = (bf16[128,2048]{1,0:T(8,128)(2,1)}, bf16[128,2048]{1,0:T(8,128)(2,1)S(1)}, u32[]{:S(2)}, u32[]{:S(2)}) collective-permute-start(bf16[128,2048]{1,0:T(8,128)(2,1)} %add_convert_fusion.1), channel_id=1, source_target_pairs={{4,0},{8,4},{12,8},{14,12},{10,14},{6,10},{2,6},{0,2},{5,1},{9,5},... | collective-permute-start | bytes 1572872 | tf_op jit(solution)/shard_map/ppermute | solution.py:790
  97.4 10.4 %collective-permute-start.20 = (bf16[64,2048]{1,0:T(8,128)(2,1)S(1)}, bf16[64,2048]{1,0:T(8,128)(2,1)S(1)}, u32[]{:S(2)}, u32[]{:S(2)}) collective-permute-start(bf16[64,2048]{1,0:T(8,128)(2,1)S(1)} %collective-permute-done.19.refs_21_), channel_id=1, source_target_pairs={{0,4},{4,8},{8,12},{12,14},{14,10},{10,6},{6,2},{2,0},{1,5},{5,9},... | collective-permute-start | bytes 786440 | tf_op jit(solution)/shard_map/ppermute | solution.py:769
  107.8 17.8 %collective-permute-start.21 = (bf16[192,2048]{1,0:T(8,128)(2,1)S(1)}, bf16[192,2048]{1,0:T(8,128)(2,1)S(1)}, u32[]{:S(2)}, u32[]{:S(2)}) collective-permute-start(bf16[192,2048]{1,0:T(8,128)(2,1)S(1)} %pad_maximum_fusion), channel_id=1, source_target_pairs={{0,16},{1,17},{2,18},{3,19},{4,20},{5,21},{6,22},{7,23},{8,24},{9,... | collective-permute-start | bytes 2359304 | tf_op jit(solution)/shard_map/ppermute | solution.py:836
  122.3 25.8 %collective-permute-start.22 = (bf16[2,2,256,256]{3,2,1,0:T(8,128)(2,1)}, bf16[2,2,256,256]{3,2,1,0:T(8,128)(2,1)S(1)}, u32[]{:S(2)}, u32[]{:S(2)}) collective-permute-start(bf16[2,2,256,256]{3,2,1,0:T(8,128)(2,1)} %get-tuple-element.99), channel_id=1, source_target_pairs={{0,1},{1,0},{2,3},{3,2},{4,5},{5,4},{6,7},{7,6},{8,9},{9,8},{10,11... | collective-permute-start | bytes 1572872 | tf_op jit(solution)/shard_map/ppermute | solution.py:865
  122.5 25.6 %collective-permute-start.24 = (bf16[128,2048]{1,0:T(8,128)(2,1)S(1)}, bf16[128,2048]{1,0:T(8,128)(2,1)S(1)}, u32[]{:S(2)}, u32[]{:S(2)}) collective-permute-start(bf16[128,2048]{1,0:T(8,128)(2,1)S(1)} %add_convert_fusion), channel_id=1, source_target_pairs={{0,4},{4,8},{8,12},{12,14},{14,10},{10,6},{6,2},{2,0},{1,5},{5,9},... | collective-permute-start | bytes 1572872 | tf_op jit(solution)/shard_map/ppermute | solution.py:866
  142.9 13.4 %all-to-all-start = ((f32[8,40,128]{2,1,0:T(8,128)}), f32[8,40,128]{2,1,0:T(8,128)S(1)}, u32[]{:S(2)}, u32[]{:S(2)}) async-start(f32[8,40,128]{2,1,0:T(8,128)} %deal.1), calls=%async_computation | async-start | bytes 327680 | tf_op jit(solution)/shard_map/all_to_all | solution.py:870
  (30 other events, 264.1 us)

commit v2 on v1

--- a/solution.py
+++ b/solution.py
@@ -395,15 +395,14 @@
         refs[1 + 2 * pairs * i : 1 + 2 * pairs * (i + 1)] for i in range(3)
     )
     refs = refs[1 + 6 * pairs :]
-    conv_refs, x_refs, w_refs = refs[:pairs], refs[pairs : 2 * pairs], refs[2 * pairs : -25]
-    direct, segment, inverse, t_ref, lag_ref = refs[-25:-20]
-    (own_ref, send_ref, stat_ref, weight, conv_buf, x_buf, ag, gs, tail, spec, xspec, taps,
-     cross, parts, os, sums, flat, w_sem, c_sem, x_sem) = refs[-20:]
+    conv_refs, x_refs, w_refs = refs[:pairs], refs[pairs : 2 * pairs], refs[2 * pairs : -27]
+    (own_ref, send_ref, stat_ref, weight, mg, conv_buf, x_buf, ag_first, ag_second, gs, tail,
+     spec, xspec, taps, cross, parts, os, flat, w_sem, c_sem, x_sem, g_sem) = refs[-22:]
+    direct, segment, inverse, t_ref, lag_ref = refs[-27:-22]
     core, offset, side_y = info[0], info[1], info[2]
     f, xh, gh, cf, ext = plan.frames, plan.xhalo, plan.ghalo, plan.chip_frames, plan.ext
     each, count = plan.back_windows
-    turn, b = pl.program_id(0), pl.program_id(1)
-    live = info[3 + b]
+    turn = pl.program_id(0)
 
     def weight_copies(pair):
         made = []
@@ -420,7 +419,7 @@
             )
         return made
 
-    def conv_copies(pair):
+    def frame_copies(pair):
         return [
             pltpu.make_async_copy(conv_refs[pair].at[i], conv_buf.at[pair, i], c_sem.at[pair, i])
             for i in range(plan.batches)
@@ -429,17 +428,33 @@
             for i in range(plan.batches)
         ]
 
-    @pl.when((turn == 0) & (b == 0))
+    def grad_copy(b):
+        return pltpu.make_async_copy(mg_ref.at[b], mg.at[b], g_sem.at[b])
+
+    def act_grad(pair, b):
+        return lax.dot_general(
+            mg[b], weight[pair], (((1,), (1,)), ((), ())), preferred_element_type=jnp.float32
+        )
+
+    @pl.when(turn == 0)
     def _():
-        for pair in range(pairs):
-            for copy in weight_copies(pair) + conv_copies(pair):
+        for copy in weight_copies(0) + [grad_copy(0)] + frame_copies(0) + [grad_copy(1)]:
+            copy.start()
+        for pair in range(1, pairs):
+            for copy in weight_copies(pair) + frame_copies(pair):
                 copy.start()
-        gs[ext:, :] = jnp.zeros((gs.shape[0] - ext, 2 * LANES), jnp.bfloat16)
-        tail[...] = jnp.zeros_like(tail)
+        for b in range(plan.batches):
+            gs[b, ext:, :] = jnp.zeros((gs.shape[1] - ext, 2 * LANES), jnp.bfloat16)
+            tail[b] = jnp.zeros(tail.shape[1:], tail.dtype)
+        for copy in weight_copies(0) + [grad_copy(0)]:
+            copy.wait()
+        ag_first[...] = act_grad(0, 0)
+        for copy in frame_copies(0) + [grad_copy(1)]:
+            copy.wait()
 
     for pair in range(pairs):
 
-        @pl.when((turn == pair) & (b == 0))
+        @pl.when(turn == pair)
         def _():
             taps[...] = taps_spectrum(t_ref, k_refs[2 * pair : 2 * pair + 2])
             for row, pick in ((0, gain_refs), (8, bias_refs)):
@@ -448,142 +463,142 @@
                     flat[row : row + 8, lanes] = jnp.broadcast_to(
                         pick[2 * pair + side][...], (8, LANES)
                     )
-            cross[...] = jnp.zeros_like(cross)
-            sums[...] = jnp.zeros_like(sums)
-            for copy in weight_copies(pair) + conv_copies(pair):
-                copy.wait()
-
+            if pair > 0:
+                for copy in frame_copies(pair):
+                    copy.wait()
+            if pair + 1 < pairs:
+                for copy in weight_copies(pair + 1):
+                    copy.wait()
+
+    gain, bias = flat[:1, :], flat[8:9, :]
     last_rows = cf - (count - 1) * each
-    for j in range(count):
-        begin = xh + j * each
-        if j < count - 1:
-            window = x_buf[turn, b, begin : begin + POINTS, :]
-        else:
-            tail[:last_rows, :] = x_buf[turn, b, begin : begin + last_rows, :]
-            window = tail[...]
-        xspec[j] = to_spectrum(segment, window)
-
-    ag[...] = lax.dot_general(
-        mg_ref[0], weight[turn], (((1,), (1,)), ((), ())), preferred_element_type=jnp.float32
-    )
-    gain, bias = flat[:1, :], flat[8:9, :]
-
+    fold = lambda v: jnp.sum(v.reshape(STEP // 8, 8, 2 * LANES), axis=0)
     gain_sum = jnp.zeros((8, 2 * LANES), jnp.float32)
     bias_sum = jnp.zeros((8, 2 * LANES), jnp.float32)
-    for row in range(0, ext, STEP):
-        conv = conv_buf[turn, b, row : row + STEP, :]
-        pre = gain * conv + bias
-        sig = sigmoid(pre)
-        value = ag[row : row + STEP, :] * sig * (1.0 + pre * (1.0 - sig))
-        gs[row : row + STEP, :] = (value * gain).astype(jnp.bfloat16)
-        if gh <= row < gh + cf:
-            fold = lambda v: jnp.sum(v.reshape(STEP // 8, 8, 2 * LANES), axis=0)
-            gain_sum = gain_sum + fold(value * conv)
-            bias_sum = bias_sum + fold(value)
-    sums[0] += gain_sum
-    sums[1] += bias_sum
-
-    for j in range(count):
-        spec[j] = to_spectrum(direct, gs[j * each : j * each + POINTS, :])
-    for j in range(count):
-        spectral_product(spec, taps, parts, j)
-        rows = min(each, cf - j * each)
-        value = from_spectrum(inverse, rows, parts, j)
-        position = offset + j * each + lax.broadcasted_iota(jnp.int32, value.shape, 0)
-        os[j * each : j * each + rows, :] = jnp.where(position < live, value, 0.0).astype(
-            jnp.bfloat16
-        )
+    for b in range(plan.batches):
+        live = info[3 + b]
+        here, ahead = (ag_first, ag_second) if b == 0 else (ag_second, ag_first)
+        following = turn if b == 0 else jnp.minimum(turn + 1, pairs - 1)
+        ahead[...] = act_grad(following, 1 - b)
+        for j in range(count):
+            begin = xh + j * each
+            if j < count - 1:
+                window = x_buf[turn, b, begin : begin + POINTS, :]
+            else:
+                tail[b, :last_rows, :] = x_buf[turn, b, begin : begin + last_rows, :]
+                window = tail[b]
+            xspec[b * count + j] = to_spectrum(segment, window)
+        for row in range(0, ext, STEP):
+            conv = conv_buf[turn, b, row : row + STEP, :]
+            pre = gain * conv + bias
+            sig = sigmoid(pre)
+            value = here[row : row + STEP, :] * sig * (1.0 + pre * (1.0 - sig))
+            gs[b, row : row + STEP, :] = (value * gain).astype(jnp.bfloat16)
+            if gh <= row < gh + cf:
+                gain_sum = gain_sum + fold(value * conv)
+                bias_sum = bias_sum + fold(value)
+        for j in range(count):
+            spec[b * count + j] = to_spectrum(direct, gs[b, j * each : j * each + POINTS, :])
+        for j in range(count):
+            slot = b * count + j
+            spectral_product(spec, taps, parts, slot)
+            rows = min(each, cf - j * each)
+            value = from_spectrum(inverse, rows, parts, slot)
+            position = offset + j * each + lax.broadcasted_iota(jnp.int32, value.shape, 0)
+            os[b, j * each : j * each + rows, :] = jnp.where(
+                position < live, value, 0.0
+            ).astype(jnp.bfloat16)
+
     for row in range(0, HALF, STEP):
         up, down = slice(row, row + STEP), slice(HALF + row, HALF + row + STEP)
-        total_r, total_i = cross[up, :], cross[down, :]
-        for j in range(count):
+        total_r = total_i = jnp.zeros((STEP, 2 * LANES), jnp.float32)
+        for j in range(plan.batches * count):
             re, im, xr, xi = spec[j, up, :], spec[j, down, :], xspec[j, up, :], xspec[j, down, :]
-            total_r = total_r + re * xr + im * xi
-            total_i = total_i + im * xr - re * xi
+            total_r = total_r + (re * xr + im * xi)
+            total_i = total_i + (im * xr - re * xi)
         cross[up, :] = total_r
         cross[down, :] = total_i
 
     @pl.when(core == 0)
     def _():
-        own_ref[0, 0] = os[:f]
-        send_ref[0, 0] = os[f:]
+        own_ref[0] = os[:, :f]
+        send_ref[0] = os[:, f:]
 
     @pl.when(core != 0)
     def _():
-        own_ref[0, 0] = os[f:]
-        send_ref[0, 0] = os[:f]
-
-    @pl.when(b == plan.batches - 1)
-    def _():
-        high, low = split(cross[...])
-        dot = functools.partial(jnp.dot, preferred_element_type=jnp.float32)
-        stat_ref[0, : plan.tap_rows] = (
-            dot(lag_ref[0], high) + dot(lag_ref[1], high) + dot(lag_ref[0], low)
-        )
-        total = [jnp.sum(sums[i], axis=0, keepdims=True) for i in range(2)]
-        pad = jnp.zeros((plan.stat_rows - plan.tap_rows - 2, 2 * LANES), jnp.float32)
-        stat_ref[0, plan.tap_rows :] = jnp.concatenate(total + [pad], axis=0)
+        own_ref[0] = os[:, f:]
+        send_ref[0] = os[:, :f]
+
+    high, low = split(cross[...])
+    dot = functools.partial(jnp.dot, preferred_element_type=jnp.float32)
+    stat_ref[0, : plan.tap_rows] = (
+        dot(lag_ref[0], high) + dot(lag_ref[1], high) + dot(lag_ref[0], low)
+    )
+    total = [jnp.sum(value, axis=0, keepdims=True) for value in (gain_sum, bias_sum)]
+    pad = jnp.zeros((plan.stat_rows - plan.tap_rows - 2, 2 * LANES), jnp.float32)
+    stat_ref[0, plan.tap_rows :] = jnp.concatenate(total + [pad], axis=0)
 
 
 def back_call(plan, steps, info, mg, sources, arrays, convs, xs, kernel, gain, bias, consts):
     bt, pairs = plan.batches, len(steps)
     direct, inverse, _, t_back, lags, segment = consts
     wide = 2 * LANES
-    slots = plan.back_windows[1]
+    slots = bt * plan.back_windows[1]
     any_space = pl.BlockSpec(memory_space=pl.ANY)
 
     def by_block(shape):
         return [
             pl.BlockSpec(
-                shape, lambda p, b, info, at=plan.block_slot(step, side): (0, info[at]),
+                shape, lambda p, info, at=plan.block_slot(step, side): (0, info[at]),
                 pipeline_mode=pl.Buffered(1),
             )
             for step in steps for side in range(2)
         ]
 
-    each = lambda *tail: pl.BlockSpec((1, 1) + tail, lambda p, b, info: (p, b, 0, 0))
+    frames = (bt, plan.frames, wide)
+    each = pl.BlockSpec((1,) + frames, lambda p, info: (p, 0, 0, 0))
     most = max(len(source) for source in sources)
     return pl.pallas_call(
         functools.partial(back_body, plan, steps, sources),
         grid_spec=pltpu.PrefetchScalarGridSpec(
             num_scalar_prefetch=1,
-            grid=(pairs, bt),
-            in_specs=[
-                pl.BlockSpec((1, plan.ext, plan.width), lambda p, b, info: (b, 0, 0)),
-            ]
+            grid=(pairs,),
+            in_specs=[any_space]
             + by_block((plan.tap_rows, LANES))
             + by_block((1, LANES))
             + by_block((1, LANES))
             + [any_space] * (2 * pairs + len(arrays))
             + [whole(c) for c in (direct, segment, inverse, t_back, lags)],
             out_specs=[
-                each(plan.frames, wide),
-                each(plan.frames, wide),
-                pl.BlockSpec((1, plan.stat_rows, wide), lambda p, b, info: (p, 0, 0)),
+                each,
+                each,
+                pl.BlockSpec((1, plan.stat_rows, wide), lambda p, info: (p, 0, 0)),
             ],
             scratch_shapes=[
                 pltpu.VMEM((pairs, wide, plan.width), jnp.bfloat16),
+                pltpu.VMEM((bt, plan.ext, plan.width), jnp.bfloat16),
                 pltpu.VMEM((pairs, bt, plan.ext, wide), jnp.float32),
                 pltpu.VMEM((pairs, bt, xs[0].shape[1], wide), jnp.bfloat16),
                 pltpu.VMEM((plan.ext, wide), jnp.float32),
-                pltpu.VMEM((plan.window_rows(plan.back_windows), wide), jnp.bfloat16),
-                pltpu.VMEM((POINTS, wide), jnp.bfloat16),
+                pltpu.VMEM((plan.ext, wide), jnp.float32),
+                pltpu.VMEM((bt, plan.window_rows(plan.back_windows), wide), jnp.bfloat16),
+                pltpu.VMEM((bt, POINTS, wide), jnp.bfloat16),
                 pltpu.VMEM((slots, POINTS, wide), jnp.float32),
                 pltpu.VMEM((slots, POINTS, wide), jnp.float32),
                 pltpu.VMEM((POINTS, wide), jnp.float32),
                 pltpu.VMEM((POINTS, wide), jnp.float32),
                 pltpu.VMEM((slots, POINTS, wide), jnp.bfloat16),
-                pltpu.VMEM((plan.chip_frames, wide), jnp.bfloat16),
-                pltpu.VMEM((2, 8, wide), jnp.float32),
+                pltpu.VMEM((bt, plan.chip_frames, wide), jnp.bfloat16),
                 pltpu.VMEM((16, wide), jnp.float32),
                 pltpu.SemaphoreType.DMA((pairs, most)),
                 pltpu.SemaphoreType.DMA((pairs, bt)),
                 pltpu.SemaphoreType.DMA((pairs, bt)),
+                pltpu.SemaphoreType.DMA((bt,)),
             ],
         ),
         out_shape=[
-            jax.ShapeDtypeStruct((pairs, bt, plan.frames, wide), jnp.bfloat16),
-            jax.ShapeDtypeStruct((pairs, bt, plan.frames, wide), jnp.bfloat16),
+            jax.ShapeDtypeStruct((pairs,) + frames, jnp.bfloat16),
+            jax.ShapeDtypeStruct((pairs,) + frames, jnp.bfloat16),
             jax.ShapeDtypeStruct((pairs, plan.stat_rows, wide), jnp.float32),
         ],
         compiler_params=pltpu.CompilerParams(vmem_limit_bytes=VMEM_LIMIT),

time: 158 us -> 158 us (level)
  no operation moved by 1% of the time
where the time goes in v2:
time: 158 us; the launch traced here: 157 us
  Pallas kernels  67.9 us (43%)
  waiting for transfers between devices  39.1 us (25%)
  starting transfers between devices  35.8 us (23%)
  local copies, waits for them, and re-layouts  8.9 us (6%)
  other arithmetic  3.35 us (2%)
  between operations  1.85 us (1%)
    pallas_call x4, Pallas kernels, conv_call(): pl.pallas_call(functools.partial(conv_body, plan), grid_spec=pltpu.Prefet...  30.3 us
    pallas_call x2, Pallas kernels, back_call(): pl.pallas_call(functools.partial(back_body, plan, steps, sources), grid_s...  24.6 us
    ppermute x4, waiting for transfers between devices, weight_round(): going[0] = lax.ppermute(going[0], 'shard', forward)  22.1 us
    ppermute x4, starting transfers between devices, weight_round(): going[0] = lax.ppermute(going[0], 'shard', forward)  8.32 us
    ppermute x1, waiting for transfers between devices, ring_shards(): xb = lax.ppermute(x_far, 'shard', plan.edges_like())  6.44 us
    unnamed x56, local copies, waits for them, and re-layouts  6.31 us
    ppermute x3, waiting for transfers between devices, weight_round(): going[1] = lax.ppermute(going[1], 'shard', backward)  6.15 us
    ppermute x3, starting transfers between devices, sum_round(): lax.ppermute(send[0], 'shard', forward)  6.1 us
  transfers between devices with their start and end apart: 26, of which 7 were waited for; matrix products, arithmetic and copies ran while one was open for 3% of the time, Pallas kernels for 39%

profile of v2, /device:TPU:0, one launch (start us, length us, event | category | flops | bytes accessed | tf_op | source)
XLA Modules:
  0.0 157.0 jit_solution(17097177472803581087)
XLA Ops:
  1.3 1.9 %edge.1 = (bf16[2,32,1024]{2,1,0:T(8,128)(2,1)}, bf16[2,32,1024]{2,1,0:T(8,128)(2,1)}, bf16[2,16,2048]{2,1,0:T(8,128)(2,1)}) custom-call(bf16[2,256,2048]{2,1,0:T(8,128)(2,1)} %refs_1_.7, bf16[2,256,2048]{2,1,0:T(8,128)(2,1)} %refs_1_.7, bf16[2,256,2048]{2,1,0:T(8,128)(2,1)} %refs_17_.8, bf16[2,256,2048]{2,1,0:T(8,128)(2,1)} %refs_17_.8), custom_call_target="tpu_custom_call" | custom-call | bytes 3600000 | tf_op jit(solution)/shard_map/edge/pallas_call | solution.py:689
  6.7 6.4 %collective-permute-done.1.refs_6_.refs_7_ = bf16[2,32,1024]{2,1,0:T(8,128)(2,1)S(1)} collective-permute-done((bf16[2,32,1024]{2,1,0:T(8,128)(2,1)}, bf16[2,32,1024]{2,1,0:T(8,128)(2,1)S(1)}, u32[]{:S(2)}, u32[]{:S(2)}) %collective-permute-start.1) | collective-permute-done | bytes 131104 | tf_op jit(solution)/shard_map/ppermute | solution.py:771
  14.5 7.4 %conv.4 = (f32[2,544,256]{2,1,0:T(8,128)}, bf16[2,640,256]{2,1,0:T(8,128)(2,1)}, bf16[128,2048]{1,0:T(8,128)(2,1)}, bf16[128,2048]{1,0:T(8,128)(2,1)}) custom-call(s32[13]{0:T(128)} %concatenate.12.info, bf16[2,256,2048]{2,1,0:T(8,128)(2,1)} %refs_1_.7, bf16[2,256,2048]{2,1,0:T(8,128)(2,1)} %refs_1_.7, bf16[2,256,2048]{2,1,0:T(8,128)(2,1)} %copy-done, ...), custom_call_target="tpu_custom_call" | custom-call | bytes 21600000 | tf_op jit(solution)/shard_map/conv/pallas_call | solution.py:350
  21.9 4.6 %collective-permute-start.4 = (bf16[128,2048]{1,0:T(8,128)(2,1)}, bf16[128,2048]{1,0:T(8,128)(2,1)S(1)}, u32[]{:S(2)}, u32[]{:S(2)}) collective-permute-start(bf16[128,2048]{1,0:T(8,128)(2,1)} %get-tuple-element.60), channel_id=1, source_target_pairs={{0,4},{4,8},{8,12},{12,14},{14,10},{10,6},{6,2},{2,0},{1,5},{5,9},... | collective-permute-start | bytes 1572872 | tf_op jit(solution)/shard_map/ppermute | solution.py:805
  28.5 4.2 %collective-permute-start.11 = (bf16[64,2048]{1,0:T(8,128)(2,1)S(1)}, bf16[64,2048]{1,0:T(8,128)(2,1)S(1)}, u32[]{:S(2)}, u32[]{:S(2)}) collective-permute-start(bf16[64,2048]{1,0:T(8,128)(2,1)S(1)} %constant_dynamic-slice_fusion), channel_id=1, source_target_pairs={{0,4},{4,8},{8,12},{12,14},{14,10},{10,6},{6,2},{2,0},{1,5},{5,9},... | collective-permute-start | bytes 786440 | tf_op jit(solution)/shard_map/ppermute | solution.py:784
  32.7 7.6 %conv.5 = (f32[2,544,256]{2,1,0:T(8,128)}, bf16[2,640,256]{2,1,0:T(8,128)(2,1)}, f32[128,2048]{1,0:T(8,128)}, f32[128,2048]{1,0:T(8,128)}) custom-call(s32[13]{0:T(128)} %concatenate.12.info, bf16[2,256,2048]{2,1,0:T(8,128)(2,1)} %refs_1_.7, bf16[2,256,2048]{2,1,0:T(8,128)(2,1)} %refs_1_.7, bf16[2,256,2048]{2,1,0:T(8,128)(2,1)} %copy-done, ...), custom_call_target="tpu_custom_call" | custom-call | bytes 21600000 | tf_op jit(solution)/shard_map/conv/pallas_call | solution.py:350
  40.3 3.8 %collective-permute-start.10 = (bf16[64,2048]{1,0:T(8,128)(2,1)S(1)}, bf16[64,2048]{1,0:T(8,128)(2,1)S(1)}, u32[]{:S(2)}, u32[]{:S(2)}) collective-permute-start(bf16[64,2048]{1,0:T(8,128)(2,1)S(1)} %constant_dynamic-slice_fusion), channel_id=1, source_target_pairs={{4,0},{8,4},{12,8},{14,12},{10,14},{6,10},{2,6},{0,2},{5,1},{9,5},... | collective-permute-start | bytes 786440 | tf_op jit(solution)/shard_map/ppermute | solution.py:787
  44.7 4.7 %assemble.1.refs_0_ = bf16[2,544,2048]{2,1,0:T(8,128)(2,1)} custom-call(s32[13]{0:T(128)} %concatenate.12.info, bf16[2,256,2048]{2,1,0:T(8,128)(2,1)} %refs_17_.8, bf16[2,256,2048]{2,1,0:T(8,128)(2,1)} %collective-permute-done.3.refs_18_.other_ref, bf16[2,16,2048]{2,1,0:T(8,128)(2,1)} %copy-done.23, bf16[2,16,2048]{2,1,0:T(8,128)(2,1)} %copy-done.24), custom_call_target="tpu_custom_call" | custom-call | bytes 18000000 | tf_op jit(solution)/shard_map/assemble/pallas_call | solution.py:734
  54.0 1.6 %collective-permute-start.12 = (bf16[128,2048]{1,0:T(8,128)(2,1)S(1)}, bf16[128,2048]{1,0:T(8,128)(2,1)S(1)}, u32[]{:S(2)}, u32[]{:S(2)}) collective-permute-start(bf16[128,2048]{1,0:T(8,128)(2,1)S(1)} %pad_maximum_fusion.1), channel_id=1, source_target_pairs={{0,16},{1,17},{2,18},{3,19},{4,20},{5,21},{6,22},{7,23},{8,24},{9,... | collective-permute-start | bytes 1572872 | tf_op jit(solution)/shard_map/ppermute | solution.py:851
  55.5 13.3 %collective-permute-done.14.refs_18_ = bf16[64,2048]{1,0:T(8,128)(2,1)S(1)} collective-permute-done((bf16[64,2048]{1,0:T(8,128)(2,1)S(1)}, bf16[64,2048]{1,0:T(8,128)(2,1)S(1)}, u32[]{:S(2)}, u32[]{:S(2)}) %collective-permute-start.14) | collective-permute-done | bytes 262176 | tf_op jit(solution)/shard_map/ppermute | solution.py:784
  69.8 1.6 %collective-permute-start.15 = (bf16[128,2048]{1,0:T(8,128)(2,1)S(1)}, bf16[128,2048]{1,0:T(8,128)(2,1)S(1)}, u32[]{:S(2)}, u32[]{:S(2)}) collective-permute-start(bf16[128,2048]{1,0:T(8,128)(2,1)S(1)} %pad_maximum_fusion.2), channel_id=1, source_target_pairs={{0,16},{1,17},{2,18},{3,19},{4,20},{5,21},{6,22},{7,23},{8,24},{9,... | collective-permute-start | bytes 1572872 | tf_op jit(solution)/shard_map/ppermute | solution.py:851
  72.8 7.6 %conv.6 = (f32[2,544,256]{2,1,0:T(8,128)}, bf16[2,640,256]{2,1,0:T(8,128)(2,1)}, f32[128,2048]{1,0:T(8,128)}, f32[128,2048]{1,0:T(8,128)}) custom-call(s32[13]{0:T(128)} %concatenate.12.info, bf16[2,256,2048]{2,1,0:T(8,128)(2,1)} %refs_1_.7, bf16[2,256,2048]{2,1,0:T(8,128)(2,1)} %refs_1_.7, bf16[2,256,2048]{2,1,0:T(8,128)(2,1)} %copy-done, ...), custom_call_target="tpu_custom_call" | custom-call | bytes 21600000 | tf_op jit(solution)/shard_map/conv/pallas_call | solution.py:350
  80.5 7.8 %conv.7 = (f32[2,544,256]{2,1,0:T(8,128)}, bf16[2,640,256]{2,1,0:T(8,128)(2,1)}, f32[128,2048]{1,0:T(8,128)}, f32[128,2048]{1,0:T(8,128)}) custom-call(s32[13]{0:T(128)} %concatenate.12.info, bf16[2,256,2048]{2,1,0:T(8,128)(2,1)} %refs_1_.7, bf16[2,256,2048]{2,1,0:T(8,128)(2,1)} %refs_1_.7, bf16[2,256,2048]{2,1,0:T(8,128)(2,1)} %copy-done, ...), custom_call_target="tpu_custom_call" | custom-call | bytes 21600000 | tf_op jit(solution)/shard_map/conv/pallas_call | solution.py:350
  89.1 1.5 collective-permute-start.16
  92.1 5.3 %collective-permute-done.18.refs_20_ = bf16[64,2048]{1,0:T(8,128)(2,1)S(1)} collective-permute-done((bf16[64,2048]{1,0:T(8,128)(2,1)S(1)}, bf16[64,2048]{1,0:T(8,128)(2,1)S(1)}, u32[]{:S(2)}, u32[]{:S(2)}) %collective-permute-start.18) | collective-permute-done | bytes 262176 | tf_op jit(solution)/shard_map/ppermute | solution.py:787
  97.4 1.6 %collective-permute-start.20 = (bf16[64,2048]{1,0:T(8,128)(2,1)S(1)}, bf16[64,2048]{1,0:T(8,128)(2,1)S(1)}, u32[]{:S(2)}, u32[]{:S(2)}) collective-permute-start(bf16[64,2048]{1,0:T(8,128)(2,1)S(1)} %collective-permute-done.19.refs_21_), channel_id=1, source_target_pairs={{0,4},{4,8},{8,12},{12,14},{14,10},{10,6},{6,2},{2,0},{1,5},{5,9},... | collective-permute-start | bytes 786440 | tf_op jit(solution)/shard_map/ppermute | solution.py:784
  99.0 8.8 %collective-permute-done.20.refs_22_ = bf16[64,2048]{1,0:T(8,128)(2,1)S(1)} collective-permute-done((bf16[64,2048]{1,0:T(8,128)(2,1)S(1)}, bf16[64,2048]{1,0:T(8,128)(2,1)S(1)}, u32[]{:S(2)}, u32[]{:S(2)}) %collective-permute-start.20) | collective-permute-done | bytes 262176 | tf_op jit(solution)/shard_map/ppermute | solution.py:784
  109.4 12.3 %back.2 = (bf16[2,2,256,256]{3,2,1,0:T(8,128)(2,1)}, bf16[2,2,256,256]{3,2,1,0:T(8,128)(2,1)}, f32[2,40,256]{2,1,0:T(8,128)}) custom-call(s32[13]{0:T(128)} %concatenate.12.info, bf16[2,544,2048]{2,1,0:T(8,128)(2,1)} %assemble.1.refs_0_, f32[32,2048]{1,0:T(8,128)} %pad.4.refs_8_.refs_9_.refs_1_.refs_2_.refs_3_.refs_4_, ...), custom_call_target="tpu_custom_call" | custom-call | bytes 43200000 | tf_op jit(solution)/shard_map/back/pallas_call | solution.py:561
  123.2 2.5 %collective-permute-done.21.refs_19_ = bf16[192,2048]{1,0:T(8,128)(2,1)S(1)} collective-permute-done((bf16[192,2048]{1,0:T(8,128)(2,1)S(1)}, bf16[192,2048]{1,0:T(8,128)(2,1)S(1)}, u32[]{:S(2)}, u32[]{:S(2)}) %collective-permute-start.21) | collective-permute-done | bytes 786464 | tf_op jit(solution)/shard_map/ppermute | solution.py:851
  126.5 12.2 %back.3 = (bf16[2,2,256,256]{3,2,1,0:T(8,128)(2,1)}, bf16[2,2,256,256]{3,2,1,0:T(8,128)(2,1)}, f32[2,40,256]{2,1,0:T(8,128)}) custom-call(s32[13]{0:T(128)} %concatenate.12.info, bf16[2,544,2048]{2,1,0:T(8,128)(2,1)} %assemble.1.refs_0_, f32[32,2048]{1,0:T(8,128)} %pad.4.refs_8_.refs_9_.refs_1_.refs_2_.refs_3_.refs_4_, ...), custom_call_target="tpu_custom_call" | custom-call | bytes 43200000 | tf_op jit(solution)/shard_map/back/pallas_call | solution.py:561
  140.2 2.3 %deal.1 = f32[8,40,128]{2,1,0:T(8,128)} custom-call(s32[13]{0:T(128)} %concatenate.12.info, f32[2,40,256]{2,1,0:T(8,128)} %get-tuple-element.84.refs_0_, f32[2,40,256]{2,1,0:T(8,128)} %get-tuple-element.97.refs_1_), custom_call_target="tpu_custom_call" | custom-call | bytes 3600000 | tf_op jit(solution)/shard_map/deal/pallas_call | solution.py:652
  142.4 5.2 %all-to-all-start = ((f32[8,40,128]{2,1,0:T(8,128)}), f32[8,40,128]{2,1,0:T(8,128)S(1)}, u32[]{:S(2)}, u32[]{:S(2)}) async-start(f32[8,40,128]{2,1,0:T(8,128)} %deal.1), calls=%async_computation | async-start | bytes 327680 | tf_op jit(solution)/shard_map/all_to_all | solution.py:885
  148.7 4.1 %place.1 = bf16[2,256,2048]{2,1,0:T(8,128)(2,1)} custom-call(s32[13]{0:T(128)} %concatenate.12.info, bf16[2,2,256,256]{3,2,1,0:T(8,128)(2,1)} %get-tuple-element.86.refs_0_, bf16[2,2,256,256]{3,2,1,0:T(8,128)(2,1)} %copy-done.20, bf16[2,2,256,256]{3,2,1,0:T(8,128)(2,1)} %get-tuple-element.100.refs_2_, bf16[2,2,256,256]{3,2,1,0:T(8,128)(2,1)} %copy-done.21), custom_call_target="tpu_custom_call" | custom-call | bytes 10800000 | tf_op jit(solution)/shard_map/place/pallas_call | solution.py:626
  153.9 1.9 %all-to-all-done = f32[8,40,128]{2,1,0:T(8,128)S(1)} async-done(((f32[8,40,128]{2,1,0:T(8,128)}), f32[8,40,128]{2,1,0:T(8,128)S(1)}, u32[]{:S(2)}, u32[]{:S(2)}) %all-to-all-start) | async-done | bytes 163872 | tf_op jit(solution)/shard_map/all_to_all | solution.py:885
  (113 shorter events, 25.0 us)
Async XLA Ops:
  0.7 12.4 %collective-permute-start.2 = (bf16[2,256,2048]{2,1,0:T(8,128)(2,1)}, bf16[2,256,2048]{2,1,0:T(8,128)(2,1)S(1)}, u32[]{:S(2)}, u32[]{:S(2)}) collective-permute-start(bf16[2,256,2048]{2,1,0:T(8,128)(2,1)} %refs_1_.7), channel_id=1, source_target_pairs={{0,1},{1,0},{2,3},{3,2},{4,5},{5,4},{6,7},{7,6},{8,9},{9,8},{10,11... | collective-permute-start | bytes 6291464 | tf_op jit(solution)/shard_map/ppermute | solution.py:772
  1.2 11.9 %collective-permute-start.3 = (bf16[2,256,2048]{2,1,0:T(8,128)(2,1)}, bf16[2,256,2048]{2,1,0:T(8,128)(2,1)}, u32[]{:S(2)}, u32[]{:S(2)}) collective-permute-start(bf16[2,256,2048]{2,1,0:T(8,128)(2,1)} %refs_17_.8), channel_id=1, source_target_pairs={{0,1},{1,0},{2,3},{3,2},{4,5},{5,4},{6,7},{7,6},{8,9},{9,8},{10,11... | collective-permute-start | bytes 6291464 | tf_op jit(solution)/shard_map/ppermute | solution.py:773
  3.9 9.2 %collective-permute-start.1 = (bf16[2,32,1024]{2,1,0:T(8,128)(2,1)}, bf16[2,32,1024]{2,1,0:T(8,128)(2,1)S(1)}, u32[]{:S(2)}, u32[]{:S(2)}) collective-permute-start(bf16[2,32,1024]{2,1,0:T(8,128)(2,1)} %get-tuple-element.55), channel_id=1, source_target_pairs={{1,3},{2,0},{3,5},{4,2},{5,7},{6,4},{7,9},{8,6},{9,11},{10,8},{11,... | collective-permute-start | bytes 393224 | tf_op jit(solution)/shard_map/ppermute | solution.py:771
  21.9 27.5 %collective-permute-start.4 = (bf16[128,2048]{1,0:T(8,128)(2,1)}, bf16[128,2048]{1,0:T(8,128)(2,1)S(1)}, u32[]{:S(2)}, u32[]{:S(2)}) collective-permute-start(bf16[128,2048]{1,0:T(8,128)(2,1)} %get-tuple-element.60), channel_id=1, source_target_pairs={{0,4},{4,8},{8,12},{12,14},{14,10},{10,6},{6,2},{2,0},{1,5},{5,9},... | collective-permute-start | bytes 1572872 | tf_op jit(solution)/shard_map/ppermute | solution.py:805
  26.5 23.0 %collective-permute-start.5 = (bf16[128,2048]{1,0:T(8,128)(2,1)}, bf16[128,2048]{1,0:T(8,128)(2,1)S(1)}, u32[]{:S(2)}, u32[]{:S(2)}) collective-permute-start(bf16[128,2048]{1,0:T(8,128)(2,1)} %get-tuple-element.64), channel_id=1, source_target_pairs={{4,0},{8,4},{12,8},{14,12},{10,14},{6,10},{2,6},{0,2},{5,1},{9,5},... | collective-permute-start | bytes 1572872 | tf_op jit(solution)/shard_map/ppermute | solution.py:805
  26.5 13.8 %collective-permute-start.6 = (bf16[2,16,2048]{2,1,0:T(8,128)(2,1)S(1)}, bf16[2,16,2048]{2,1,0:T(8,128)(2,1)S(1)}, u32[]{:S(2)}, u32[]{:S(2)}) collective-permute-start(bf16[2,16,2048]{2,1,0:T(8,128)(2,1)S(1)} %copy-done.27), channel_id=1, source_target_pairs={{1,2},{2,1},{3,4},{4,3},{5,6},{6,5},{7,8},{8,7},{9,10},{10,9},{11,... | collective-permute-start | bytes 393224 | tf_op jit(solution)/shard_map/ppermute | solution.py:820
  27.1 16.9 %collective-permute-start.7 = (bf16[2,16,2048]{2,1,0:T(8,128)(2,1)S(1)}, bf16[2,16,2048]{2,1,0:T(8,128)(2,1)S(1)}, u32[]{:S(2)}, u32[]{:S(2)}) collective-permute-start(bf16[2,16,2048]{2,1,0:T(8,128)(2,1)S(1)} %copy-done.27), channel_id=1, source_target_pairs={{1,3},{2,0},{3,5},{4,2},{5,7},{6,4},{7,9},{8,6},{9,11},{10,8},{11,... | collective-permute-start | bytes 393224 | tf_op jit(solution)/shard_map/ppermute | solution.py:821
  28.5 23.3 %collective-permute-start.11 = (bf16[64,2048]{1,0:T(8,128)(2,1)S(1)}, bf16[64,2048]{1,0:T(8,128)(2,1)S(1)}, u32[]{:S(2)}, u32[]{:S(2)}) collective-permute-start(bf16[64,2048]{1,0:T(8,128)(2,1)S(1)} %constant_dynamic-slice_fusion), channel_id=1, source_target_pairs={{0,4},{4,8},{8,12},{12,14},{14,10},{10,6},{6,2},{2,0},{1,5},{5,9},... | collective-permute-start | bytes 786440 | tf_op jit(solution)/shard_map/ppermute | solution.py:784
  40.3 11.5 %collective-permute-start.10 = (bf16[64,2048]{1,0:T(8,128)(2,1)S(1)}, bf16[64,2048]{1,0:T(8,128)(2,1)S(1)}, u32[]{:S(2)}, u32[]{:S(2)}) collective-permute-start(bf16[64,2048]{1,0:T(8,128)(2,1)S(1)} %constant_dynamic-slice_fusion), channel_id=1, source_target_pairs={{4,0},{8,4},{12,8},{14,12},{10,14},{6,10},{2,6},{0,2},{5,1},{9,5},... | collective-permute-start | bytes 786440 | tf_op jit(solution)/shard_map/ppermute | solution.py:787
  49.6 38.7 %collective-permute-start.8 = (bf16[128,2048]{1,0:T(8,128)(2,1)S(1)}, bf16[128,2048]{1,0:T(8,128)(2,1)S(1)}, u32[]{:S(2)}, u32[]{:S(2)}) collective-permute-start(bf16[128,2048]{1,0:T(8,128)(2,1)S(1)} %add_convert_fusion.4), channel_id=1, source_target_pairs={{0,4},{4,8},{8,12},{12,14},{14,10},{10,6},{6,2},{2,0},{1,5},{5,9},... | collective-permute-start | bytes 1572872 | tf_op jit(solution)/shard_map/ppermute | solution.py:805
  50.8 38.2 %collective-permute-start.9 = (bf16[128,2048]{1,0:T(8,128)(2,1)S(1)}, bf16[128,2048]{1,0:T(8,128)(2,1)S(1)}, u32[]{:S(2)}, u32[]{:S(2)}) collective-permute-start(bf16[128,2048]{1,0:T(8,128)(2,1)S(1)} %add_convert_fusion.3), channel_id=1, source_target_pairs={{4,0},{8,4},{12,8},{14,12},{10,14},{6,10},{2,6},{0,2},{5,1},{9,5},... | collective-permute-start | bytes 1572872 | tf_op jit(solution)/shard_map/ppermute | solution.py:805
  51.8 17.1 %collective-permute-start.14 = (bf16[64,2048]{1,0:T(8,128)(2,1)S(1)}, bf16[64,2048]{1,0:T(8,128)(2,1)S(1)}, u32[]{:S(2)}, u32[]{:S(2)}) collective-permute-start(bf16[64,2048]{1,0:T(8,128)(2,1)S(1)} %collective-permute-done.11.refs_20_), channel_id=1, source_target_pairs={{0,4},{4,8},{8,12},{12,14},{14,10},{10,6},{6,2},{2,0},{1,5},{5,9},... | collective-permute-start | bytes 786440 | tf_op jit(solution)/shard_map/ppermute | solution.py:784
  52.9 16.8 %collective-permute-start.13 = (bf16[64,2048]{1,0:T(8,128)(2,1)S(1)}, bf16[64,2048]{1,0:T(8,128)(2,1)S(1)}, u32[]{:S(2)}, u32[]{:S(2)}) collective-permute-start(bf16[64,2048]{1,0:T(8,128)(2,1)S(1)} %collective-permute-done.10.refs_19_), channel_id=1, source_target_pairs={{4,0},{8,4},{12,8},{14,12},{10,14},{6,10},{2,6},{0,2},{5,1},{9,5},... | collective-permute-start | bytes 786440 | tf_op jit(solution)/shard_map/ppermute | solution.py:787
  54.0 54.5 %collective-permute-start.12 = (bf16[128,2048]{1,0:T(8,128)(2,1)S(1)}, bf16[128,2048]{1,0:T(8,128)(2,1)S(1)}, u32[]{:S(2)}, u32[]{:S(2)}) collective-permute-start(bf16[128,2048]{1,0:T(8,128)(2,1)S(1)} %pad_maximum_fusion.1), channel_id=1, source_target_pairs={{0,16},{1,17},{2,18},{3,19},{4,20},{5,21},{6,22},{7,23},{8,24},{9,... | collective-permute-start | bytes 1572872 | tf_op jit(solution)/shard_map/ppermute | solution.py:851
  69.8 38.7 %collective-permute-start.15 = (bf16[128,2048]{1,0:T(8,128)(2,1)S(1)}, bf16[128,2048]{1,0:T(8,128)(2,1)S(1)}, u32[]{:S(2)}, u32[]{:S(2)}) collective-permute-start(bf16[128,2048]{1,0:T(8,128)(2,1)S(1)} %pad_maximum_fusion.2), channel_id=1, source_target_pairs={{0,16},{1,17},{2,18},{3,19},{4,20},{5,21},{6,22},{7,23},{8,24},{9,... | collective-permute-start | bytes 1572872 | tf_op jit(solution)/shard_map/ppermute | solution.py:851
  71.4 20.1 %collective-permute-start.19 = (bf16[64,2048]{1,0:T(8,128)(2,1)S(1)}, bf16[64,2048]{1,0:T(8,128)(2,1)S(1)}, u32[]{:S(2)}, u32[]{:S(2)}) collective-permute-start(bf16[64,2048]{1,0:T(8,128)(2,1)S(1)} %collective-permute-done.14.refs_18_), channel_id=1, source_target_pairs={{0,4},{4,8},{8,12},{12,14},{14,10},{10,6},{6,2},{2,0},{1,5},{5,9},... | collective-permute-start | bytes 786440 | tf_op jit(solution)/shard_map/ppermute | solution.py:784
  88.3 9.1 %collective-permute-start.18 = (bf16[64,2048]{1,0:T(8,128)(2,1)S(1)}, bf16[64,2048]{1,0:T(8,128)(2,1)S(1)}, u32[]{:S(2)}, u32[]{:S(2)}) collective-permute-start(bf16[64,2048]{1,0:T(8,128)(2,1)S(1)} %collective-permute-done.13.refs_22_), channel_id=1, source_target_pairs={{4,0},{8,4},{12,8},{14,12},{10,14},{6,10},{2,6},{0,2},{5,1},{9,5},... | collective-permute-start | bytes 786440 | tf_op jit(solution)/shard_map/ppermute | solution.py:787
  89.1 32.8 %collective-permute-start.16 = (bf16[128,2048]{1,0:T(8,128)(2,1)S(1)}, bf16[128,2048]{1,0:T(8,128)(2,1)S(1)}, u32[]{:S(2)}, u32[]{:S(2)}) collective-permute-start(bf16[128,2048]{1,0:T(8,128)(2,1)S(1)} %add_convert_fusion.2), channel_id=1, source_target_pairs={{0,4},{4,8},{8,12},{12,14},{14,10},{10,6},{6,2},{2,0},{1,5},{5,9},... | collective-permute-start | bytes 1572872 | tf_op jit(solution)/shard_map/ppermute | solution.py:805
  91.4 30.5 %collective-permute-start.17 = (bf16[128,2048]{1,0:T(8,128)(2,1)}, bf16[128,2048]{1,0:T(8,128)(2,1)S(1)}, u32[]{:S(2)}, u32[]{:S(2)}) collective-permute-start(bf16[128,2048]{1,0:T(8,128)(2,1)} %add_convert_fusion.1), channel_id=1, source_target_pairs={{4,0},{8,4},{12,8},{14,12},{10,14},{6,10},{2,6},{0,2},{5,1},{9,5},... | collective-permute-start | bytes 1572872 | tf_op jit(solution)/shard_map/ppermute | solution.py:805
  97.4 10.4 %collective-permute-start.20 = (bf16[64,2048]{1,0:T(8,128)(2,1)S(1)}, bf16[64,2048]{1,0:T(8,128)(2,1)S(1)}, u32[]{:S(2)}, u32[]{:S(2)}) collective-permute-start(bf16[64,2048]{1,0:T(8,128)(2,1)S(1)} %collective-permute-done.19.refs_21_), channel_id=1, source_target_pairs={{0,4},{4,8},{8,12},{12,14},{14,10},{10,6},{6,2},{2,0},{1,5},{5,9},... | collective-permute-start | bytes 786440 | tf_op jit(solution)/shard_map/ppermute | solution.py:784
  107.8 17.8 %collective-permute-start.21 = (bf16[192,2048]{1,0:T(8,128)(2,1)S(1)}, bf16[192,2048]{1,0:T(8,128)(2,1)S(1)}, u32[]{:S(2)}, u32[]{:S(2)}) collective-permute-start(bf16[192,2048]{1,0:T(8,128)(2,1)S(1)} %pad_maximum_fusion), channel_id=1, source_target_pairs={{0,16},{1,17},{2,18},{3,19},{4,20},{5,21},{6,22},{7,23},{8,24},{9,... | collective-permute-start | bytes 2359304 | tf_op jit(solution)/shard_map/ppermute | solution.py:851
  121.8 25.9 %collective-permute-start.22 = (bf16[2,2,256,256]{3,2,1,0:T(8,128)(2,1)}, bf16[2,2,256,256]{3,2,1,0:T(8,128)(2,1)S(1)}, u32[]{:S(2)}, u32[]{:S(2)}) collective-permute-start(bf16[2,2,256,256]{3,2,1,0:T(8,128)(2,1)} %get-tuple-element.99), channel_id=1, source_target_pairs={{0,1},{1,0},{2,3},{3,2},{4,5},{5,4},{6,7},{7,6},{8,9},{9,8},{10,11... | collective-permute-start | bytes 1572872 | tf_op jit(solution)/shard_map/ppermute | solution.py:880
  122.1 25.6 %collective-permute-start.24 = (bf16[128,2048]{1,0:T(8,128)(2,1)S(1)}, bf16[128,2048]{1,0:T(8,128)(2,1)S(1)}, u32[]{:S(2)}, u32[]{:S(2)}) collective-permute-start(bf16[128,2048]{1,0:T(8,128)(2,1)S(1)} %add_convert_fusion), channel_id=1, source_target_pairs={{0,4},{4,8},{8,12},{12,14},{14,10},{10,6},{6,2},{2,0},{1,5},{5,9},... | collective-permute-start | bytes 1572872 | tf_op jit(solution)/shard_map/ppermute | solution.py:881
  142.4 13.4 %all-to-all-start = ((f32[8,40,128]{2,1,0:T(8,128)}), f32[8,40,128]{2,1,0:T(8,128)S(1)}, u32[]{:S(2)}, u32[]{:S(2)}) async-start(f32[8,40,128]{2,1,0:T(8,128)} %deal.1), calls=%async_computation | async-start | bytes 327680 | tf_op jit(solution)/shard_map/all_to_all | solution.py:885
  (30 other events, 262.1 us)
